TPU v7x, 1024 devices: a whole 4x8x16 slice. The times are simulated.
1024 devices in a mesh: inst: 16 (over z_lo, x), dom: 64 (over y, z_hi, core).
Axes of the slice: x: 4, y: 8, z: 16 (z_hi: 4, z_lo: 4; z = z_hi * 4 + z_lo), core: 2. Of those that a mesh axis runs over, the one named last changes fastest.
Arguments:
- perturbation: float32 [16, 6, 1024, 1024], P('inst', None, 'dom'), may hold values from -6 to 6
- jacobian: float32 [16, 6, 6, 1024, 1024], P('inst', None, None, 'dom'), may hold values from -2.5 to 2.5
- flux_theta: float32 [6, 6], replicated, may hold values from -2.5 to 2.5
- flux_merid: float32 [6, 6], replicated, may hold values from -2.5 to 2.5
- donor_rows: int32 [16, 2, 1024], P('inst', None, 'dom'), may hold values from 0 to 1023
- donor_weights: float32 [16, 2, 1024], P('inst', None, 'dom'), may hold values from 0 to 1
Outputs:
- product: float32 [16, 6, 1024, 1024], P('inst', None, 'dom')
Inputs may be any that keep to these rules, and one draw needn't show every extreme that they name: `donor_rows`: donor lines are global circumferential indices on the outlet face.
All inputs are finite; a program needn't handle non-finite values.
Results may differ from a plain program's by a relative error of at most 0.0014.
The roundings to bfloat16 on the way count: a program that leaves them out, or rounds other values in their place, can miss the bound.
Values may be sent and summed in bfloat16 or wider, within the bound.
No kernel may reach another device: no remote copies, remote signals or barrier semaphores. Data moves between devices by JAX's collectives and lax.ppermute only.
A program may use at most 32 MiB of HBM per device.

v0:
```python
import jax
import jax.numpy as jnp
from jax import lax
from jax.sharding import PartitionSpec as P

OMEGA = 0.5
NYQUIST = 2.0


def passed_along(value, axis, steps):
    count = lax.axis_size(axis)
    pairs = [(source, (source + steps) % count) for source in range(count)]
    return lax.ppermute(value, axis, pairs)


def padded_2(cells, sides, width):
    for axis, dim in sides:
        count = lax.axis_size(axis)
        head = lax.slice_in_dim(cells, 0, width, axis=dim)
        tail = lax.slice_in_dim(cells, cells.shape[dim] - width, cells.shape[dim], axis=dim)
        cells = jnp.concatenate(
            [
                lax.ppermute(tail, axis, [(i, (i + 1) % count) for i in range(count)]),
                cells,
                lax.ppermute(head, axis, [((i + 1) % count, i) for i in range(count)]),
            ],
            axis=dim,
        )
    return cells


def spectral_row(count):
    offs = jnp.arange(count, dtype=jnp.int32)
    sign = (1 - 2 * (offs % 2)).astype(jnp.float32)
    safe = jnp.maximum(offs, 1).astype(jnp.float32)
    angle = jnp.pi * safe / count
    cotan = jnp.where(offs == 0, 0.0, jnp.cos(angle) / jnp.sin(angle))
    return OMEGA * 0.5 * sign * cotan + NYQUIST * sign / count


def shards(perturbation, jacobian, flux_theta, flux_merid, donor_rows, donor_weights):
    count = lax.axis_size("inst")
    table = spectral_row(count)
    low = perturbation.astype(jnp.bfloat16)
    correction = table[0] * (perturbation - low.astype(jnp.float32))

    def forward_step(step, carry):
        piece, total = carry
        piece = passed_along(piece, "inst", 1)
        return (piece, total + table[step] * piece.astype(jnp.float32))

    start_total = table[0] * low.astype(jnp.float32)
    moved, temporal = lax.fori_loop(1, count, forward_step, (low, start_total))
    temporal = temporal + correction
    padded = padded_2(perturbation, (("dom", 2),), 1)
    dtheta = padded[:, :, 2:, :] - padded[:, :, :-2, :]
    merid_pad = jnp.pad(perturbation, ((0, 0), (0, 0), (0, 0), (1, 1)))
    dmerid = merid_pad[:, :, :, 2:] - merid_pad[:, :, :, :-2]
    spatial = jnp.einsum(
        "iabtm,ibtm->iatm", jacobian, perturbation, precision=lax.Precision.HIGHEST
    )
    spatial = spatial + jnp.einsum(
        "ab,ibtm->iatm", flux_theta, dtheta, precision=lax.Precision.HIGHEST
    )
    spatial = spatial + jnp.einsum(
        "ab,ibtm->iatm", flux_merid, dmerid, precision=lax.Precision.HIGHEST
    )
    last_cell = perturbation.shape[3] - 1
    outlet = lax.all_gather(perturbation[0, :, :, last_cell], "dom", axis=1, tiled=True)
    interp = jnp.zeros((perturbation.shape[1], perturbation.shape[2]), jnp.float32)
    for donor in range(2):
        picked = jnp.take(outlet, donor_rows[0, donor], axis=1)
        interp = interp + donor_weights[0, donor][None, :] * picked
    interface = perturbation[0, :, :, 0] - interp
    product = temporal + spatial
    return product.at[0, :, :, 0].add(interface)


def solution(mesh):
    in_specs = (
        P("inst", None, "dom", None),
        P("inst", None, None, "dom", None),
        P(),
        P(),
        P("inst", None, "dom"),
        P("inst", None, "dom"),
    )
    out_specs = P("inst", None, "dom", None)
    return jax.shard_map(shards, mesh=mesh, in_specs=in_specs, out_specs=out_specs, check_vma=False)
```

profile of v0, /device:TPU:32, one launch (start us, length us, event | category | flops | bytes accessed | tf_op | source)
XLA Modules:
  0.0 321.1 jit_solution(14136001316747420860)
XLA Ops:
  1.1 1.9 collective-permute-start.2
  3.0 17.5 %collective-permute-start.1 = (f32[1,6,1,1024]{3,2,1,0:T(1,128)S(1)}, f32[1,6,1,1024]{3,2,1,0:T(1,128)S(1)}, u32[]{:S(2)}, u32[]{:S(2)}) collective-permute-start(f32[1,6,1,1024]{3,2,1,0:T(1,128)S(1)} %get-tuple-element.153), channel_id=1, source_target_pairs={{1,0},{2,1},{3,2},{4,3},{5,4},{6,5},{7,6},{8,7},{9,8},{10,9},{11,1... | collective-permute-start | bytes 73736 | tf_op jit(solution)/shard_map/ppermute | solution.py:25
  23.1 98.4 %all-gather = f32[1,6,1024,1]{1,2,3,0:T(8,128)S(1)} all-gather(f32[1,6,16,1]{1,2,3,0:T(8,128)S(1)} %copy.42), channel_id=2, replica_groups=mesh['inst'=16,'dom'=64] {'dom'}, dimensions={2}, use_global_device_ids=true | all-gather | bytes 24960 | tf_op jit(solution)/shard_map/all_gather | solution.py:69
  124.4 2.1 fusion
  128.5 190.1 %while.18 = (s32[]{:T(128)}, bf16[1,6,16,1024]{3,2,1,0:T(8,128)(2,1)S(1)}, f32[1,6,16,1024]{3,2,1,0:T(8,128)S(1)}, f32[16]{0:T(128)S(1)}, s32[]{:T(128)}, /*index=5*/s32[]{:T(128)}, s32[]{:T(128)}) while((s32[]{:T(128)}, bf16[1,6,16,1024]{3,2,1,0:T(8,128)(2,1)S(1)}, f32[1,6,16,1024]{3,2,1,0:T(8,128)S(1)}, f32[16]{0:T(128)S(1)}, s32[]{:T(128)}, ...), condition=%wide.region_1.2_spmd, body=%wide.region_0.1_spmd.sunk | while | flops 294917 | bytes 2162863 | solution.py:53
  128.5 3.4 %collective-permute-start = (bf16[1,6,16,1024]{3,2,1,0:T(8,128)(2,1)S(1)}, bf16[1,6,16,1024]{3,2,1,0:T(8,128)(2,1)S(1)}, u32[]{:S(2)}, u32[]{:S(2)}) collective-permute-start(bf16[1,6,16,1024]{3,2,1,0:T(8,128)(2,1)S(1)} %get-tuple-element.194), channel_id=1, source_target_pairs={{0,64},{64,128},{128,192},{192,256},{256,320},{320,384},{384,448},... | collective-permute-start | bytes 589832 | tf_op jit(solution)/shard_map/while/body/eval_jaxpr/ppermute | solution.py:13
  132.5 9.0 %collective-permute-done = bf16[1,6,16,1024]{3,2,1,0:T(8,128)(2,1)S(1)} collective-permute-done((bf16[1,6,16,1024]{3,2,1,0:T(8,128)(2,1)S(1)}, bf16[1,6,16,1024]{3,2,1,0:T(8,128)(2,1)S(1)}, u32[]{:S(2)}, u32[]{:S(2)}) %collective-permute-start) | collective-permute-done | bytes 196640 | tf_op jit(solution)/shard_map/while/body/eval_jaxpr/ppermute | solution.py:13
  142.3 1.9 collective-permute-start
  144.9 9.7 %collective-permute-done = bf16[1,6,16,1024]{3,2,1,0:T(8,128)(2,1)S(1)} collective-permute-done((bf16[1,6,16,1024]{3,2,1,0:T(8,128)(2,1)S(1)}, bf16[1,6,16,1024]{3,2,1,0:T(8,128)(2,1)S(1)}, u32[]{:S(2)}, u32[]{:S(2)}) %collective-permute-start) | collective-permute-done | bytes 196640 | tf_op jit(solution)/shard_map/while/body/eval_jaxpr/ppermute | solution.py:13
  155.3 1.9 collective-permute-start
  157.9 8.9 %collective-permute-done = bf16[1,6,16,1024]{3,2,1,0:T(8,128)(2,1)S(1)} collective-permute-done((bf16[1,6,16,1024]{3,2,1,0:T(8,128)(2,1)S(1)}, bf16[1,6,16,1024]{3,2,1,0:T(8,128)(2,1)S(1)}, u32[]{:S(2)}, u32[]{:S(2)}) %collective-permute-start) | collective-permute-done | bytes 196640 | tf_op jit(solution)/shard_map/while/body/eval_jaxpr/ppermute | solution.py:13
  167.6 1.9 collective-permute-start
  170.1 8.9 %collective-permute-done = bf16[1,6,16,1024]{3,2,1,0:T(8,128)(2,1)S(1)} collective-permute-done((bf16[1,6,16,1024]{3,2,1,0:T(8,128)(2,1)S(1)}, bf16[1,6,16,1024]{3,2,1,0:T(8,128)(2,1)S(1)}, u32[]{:S(2)}, u32[]{:S(2)}) %collective-permute-start) | collective-permute-done | bytes 196640 | tf_op jit(solution)/shard_map/while/body/eval_jaxpr/ppermute | solution.py:13
  179.8 1.9 collective-permute-start
  182.4 8.9 %collective-permute-done = bf16[1,6,16,1024]{3,2,1,0:T(8,128)(2,1)S(1)} collective-permute-done((bf16[1,6,16,1024]{3,2,1,0:T(8,128)(2,1)S(1)}, bf16[1,6,16,1024]{3,2,1,0:T(8,128)(2,1)S(1)}, u32[]{:S(2)}, u32[]{:S(2)}) %collective-permute-start) | collective-permute-done | bytes 196640 | tf_op jit(solution)/shard_map/while/body/eval_jaxpr/ppermute | solution.py:13
  192.1 1.9 collective-permute-start
  194.6 8.9 %collective-permute-done = bf16[1,6,16,1024]{3,2,1,0:T(8,128)(2,1)S(1)} collective-permute-done((bf16[1,6,16,1024]{3,2,1,0:T(8,128)(2,1)S(1)}, bf16[1,6,16,1024]{3,2,1,0:T(8,128)(2,1)S(1)}, u32[]{:S(2)}, u32[]{:S(2)}) %collective-permute-start) | collective-permute-done | bytes 196640 | tf_op jit(solution)/shard_map/while/body/eval_jaxpr/ppermute | solution.py:13
  204.3 1.9 collective-permute-start
  206.8 8.9 %collective-permute-done = bf16[1,6,16,1024]{3,2,1,0:T(8,128)(2,1)S(1)} collective-permute-done((bf16[1,6,16,1024]{3,2,1,0:T(8,128)(2,1)S(1)}, bf16[1,6,16,1024]{3,2,1,0:T(8,128)(2,1)S(1)}, u32[]{:S(2)}, u32[]{:S(2)}) %collective-permute-start) | collective-permute-done | bytes 196640 | tf_op jit(solution)/shard_map/while/body/eval_jaxpr/ppermute | solution.py:13
  216.5 1.9 collective-permute-start
  219.1 8.9 %collective-permute-done = bf16[1,6,16,1024]{3,2,1,0:T(8,128)(2,1)S(1)} collective-permute-done((bf16[1,6,16,1024]{3,2,1,0:T(8,128)(2,1)S(1)}, bf16[1,6,16,1024]{3,2,1,0:T(8,128)(2,1)S(1)}, u32[]{:S(2)}, u32[]{:S(2)}) %collective-permute-start) | collective-permute-done | bytes 196640 | tf_op jit(solution)/shard_map/while/body/eval_jaxpr/ppermute | solution.py:13
  228.8 1.9 collective-permute-start
  231.3 9.0 %collective-permute-done = bf16[1,6,16,1024]{3,2,1,0:T(8,128)(2,1)S(1)} collective-permute-done((bf16[1,6,16,1024]{3,2,1,0:T(8,128)(2,1)S(1)}, bf16[1,6,16,1024]{3,2,1,0:T(8,128)(2,1)S(1)}, u32[]{:S(2)}, u32[]{:S(2)}) %collective-permute-start) | collective-permute-done | bytes 196640 | tf_op jit(solution)/shard_map/while/body/eval_jaxpr/ppermute | solution.py:13
  241.1 1.9 collective-permute-start
  243.7 10.2 %collective-permute-done = bf16[1,6,16,1024]{3,2,1,0:T(8,128)(2,1)S(1)} collective-permute-done((bf16[1,6,16,1024]{3,2,1,0:T(8,128)(2,1)S(1)}, bf16[1,6,16,1024]{3,2,1,0:T(8,128)(2,1)S(1)}, u32[]{:S(2)}, u32[]{:S(2)}) %collective-permute-start) | collective-permute-done | bytes 196640 | tf_op jit(solution)/shard_map/while/body/eval_jaxpr/ppermute | solution.py:13
  254.6 1.9 collective-permute-start
  257.1 10.7 %collective-permute-done = bf16[1,6,16,1024]{3,2,1,0:T(8,128)(2,1)S(1)} collective-permute-done((bf16[1,6,16,1024]{3,2,1,0:T(8,128)(2,1)S(1)}, bf16[1,6,16,1024]{3,2,1,0:T(8,128)(2,1)S(1)}, u32[]{:S(2)}, u32[]{:S(2)}) %collective-permute-start) | collective-permute-done | bytes 196640 | tf_op jit(solution)/shard_map/while/body/eval_jaxpr/ppermute | solution.py:13
  271.2 9.9 %collective-permute-done = bf16[1,6,16,1024]{3,2,1,0:T(8,128)(2,1)S(1)} collective-permute-done((bf16[1,6,16,1024]{3,2,1,0:T(8,128)(2,1)S(1)}, bf16[1,6,16,1024]{3,2,1,0:T(8,128)(2,1)S(1)}, u32[]{:S(2)}, u32[]{:S(2)}) %collective-permute-start) | collective-permute-done | bytes 196640 | tf_op jit(solution)/shard_map/while/body/eval_jaxpr/ppermute | solution.py:13
  281.9 1.9 collective-permute-start
  284.4 9.0 %collective-permute-done = bf16[1,6,16,1024]{3,2,1,0:T(8,128)(2,1)S(1)} collective-permute-done((bf16[1,6,16,1024]{3,2,1,0:T(8,128)(2,1)S(1)}, bf16[1,6,16,1024]{3,2,1,0:T(8,128)(2,1)S(1)}, u32[]{:S(2)}, u32[]{:S(2)}) %collective-permute-start) | collective-permute-done | bytes 196640 | tf_op jit(solution)/shard_map/while/body/eval_jaxpr/ppermute | solution.py:13
  296.7 8.9 %collective-permute-done = bf16[1,6,16,1024]{3,2,1,0:T(8,128)(2,1)S(1)} collective-permute-done((bf16[1,6,16,1024]{3,2,1,0:T(8,128)(2,1)S(1)}, bf16[1,6,16,1024]{3,2,1,0:T(8,128)(2,1)S(1)}, u32[]{:S(2)}, u32[]{:S(2)}) %collective-permute-start) | collective-permute-done | bytes 196640 | tf_op jit(solution)/shard_map/while/body/eval_jaxpr/ppermute | solution.py:13
  309.0 8.9 %collective-permute-done = bf16[1,6,16,1024]{3,2,1,0:T(8,128)(2,1)S(1)} collective-permute-done((bf16[1,6,16,1024]{3,2,1,0:T(8,128)(2,1)S(1)}, bf16[1,6,16,1024]{3,2,1,0:T(8,128)(2,1)S(1)}, u32[]{:S(2)}, u32[]{:S(2)}) %collective-permute-start) | collective-permute-done | bytes 196640 | tf_op jit(solution)/shard_map/while/body/eval_jaxpr/ppermute | solution.py:13
  (80 shorter events, 37.0 us)
Async XLA Ops:
  0.0 127.5 %copy-start = (f32[6,6]{1,0:T(8,128)S(1)}, f32[6,6]{1,0:T(8,128)}, u32[]{:S(2)}) copy-start(f32[6,6]{1,0:T(8,128)} %param.14) | copy-start | bytes 436
  1.1 126.1 %collective-permute-start.2 = (f32[1,6,1,1024]{3,2,1,0:T(1,128)S(1)}, f32[1,6,1,1024]{3,2,1,0:T(1,128)S(1)}, u32[]{:S(2)}, u32[]{:S(2)}) collective-permute-start(f32[1,6,1,1024]{3,2,1,0:T(1,128)S(1)} %get-tuple-element.154), channel_id=1, source_target_pairs={{0,1},{1,2},{2,3},{3,4},{4,5},{5,6},{6,7},{7,8},{8,9},{9,10},{10,1... | collective-permute-start | bytes 73736 | tf_op jit(solution)/shard_map/ppermute | solution.py:23
  3.0 124.2 %collective-permute-start.1 = (f32[1,6,1,1024]{3,2,1,0:T(1,128)S(1)}, f32[1,6,1,1024]{3,2,1,0:T(1,128)S(1)}, u32[]{:S(2)}, u32[]{:S(2)}) collective-permute-start(f32[1,6,1,1024]{3,2,1,0:T(1,128)S(1)} %get-tuple-element.153), channel_id=1, source_target_pairs={{1,0},{2,1},{3,2},{4,3},{5,4},{6,5},{7,6},{8,7},{9,8},{10,9},{11,1... | collective-permute-start | bytes 73736 | tf_op jit(solution)/shard_map/ppermute | solution.py:25
  21.5 105.0 %copy-start.1 = (f32[1,6,16,1024]{3,2,1,0:T(8,128)S(1)}, f32[1,6,16,1024]{3,2,1,0:T(8,128)}, u32[]{:S(2)}) copy-start(f32[1,6,16,1024]{3,2,1,0:T(8,128)} %param.12) | copy-start | bytes 1179652
  128.5 190.2 %copy-start.2 = (f32[6,6]{1,0:T(8,128)S(1)}, f32[6,6]{1,0:T(8,128)}, u32[]{:S(2)}) copy-start(f32[6,6]{1,0:T(8,128)} %param.15) | copy-start | bytes 436
  128.5 13.0 %collective-permute-start = (bf16[1,6,16,1024]{3,2,1,0:T(8,128)(2,1)S(1)}, bf16[1,6,16,1024]{3,2,1,0:T(8,128)(2,1)S(1)}, u32[]{:S(2)}, u32[]{:S(2)}) collective-permute-start(bf16[1,6,16,1024]{3,2,1,0:T(8,128)(2,1)S(1)} %get-tuple-element.194), channel_id=1, source_target_pairs={{0,64},{64,128},{128,192},{192,256},{256,320},{320,384},{384,448},... | collective-permute-start | bytes 589832 | tf_op jit(solution)/shard_map/while/body/eval_jaxpr/ppermute | solution.py:13
  142.3 12.2 %collective-permute-start = (bf16[1,6,16,1024]{3,2,1,0:T(8,128)(2,1)S(1)}, bf16[1,6,16,1024]{3,2,1,0:T(8,128)(2,1)S(1)}, u32[]{:S(2)}, u32[]{:S(2)}) collective-permute-start(bf16[1,6,16,1024]{3,2,1,0:T(8,128)(2,1)S(1)} %get-tuple-element.194), channel_id=1, source_target_pairs={{0,64},{64,128},{128,192},{192,256},{256,320},{320,384},{384,448},... | collective-permute-start | bytes 589832 | tf_op jit(solution)/shard_map/while/body/eval_jaxpr/ppermute | solution.py:13
  155.3 11.5 %collective-permute-start = (bf16[1,6,16,1024]{3,2,1,0:T(8,128)(2,1)S(1)}, bf16[1,6,16,1024]{3,2,1,0:T(8,128)(2,1)S(1)}, u32[]{:S(2)}, u32[]{:S(2)}) collective-permute-start(bf16[1,6,16,1024]{3,2,1,0:T(8,128)(2,1)S(1)} %get-tuple-element.194), channel_id=1, source_target_pairs={{0,64},{64,128},{128,192},{192,256},{256,320},{320,384},{384,448},... | collective-permute-start | bytes 589832 | tf_op jit(solution)/shard_map/while/body/eval_jaxpr/ppermute | solution.py:13
  167.6 11.5 %collective-permute-start = (bf16[1,6,16,1024]{3,2,1,0:T(8,128)(2,1)S(1)}, bf16[1,6,16,1024]{3,2,1,0:T(8,128)(2,1)S(1)}, u32[]{:S(2)}, u32[]{:S(2)}) collective-permute-start(bf16[1,6,16,1024]{3,2,1,0:T(8,128)(2,1)S(1)} %get-tuple-element.194), channel_id=1, source_target_pairs={{0,64},{64,128},{128,192},{192,256},{256,320},{320,384},{384,448},... | collective-permute-start | bytes 589832 | tf_op jit(solution)/shard_map/while/body/eval_jaxpr/ppermute | solution.py:13
  179.8 11.5 %collective-permute-start = (bf16[1,6,16,1024]{3,2,1,0:T(8,128)(2,1)S(1)}, bf16[1,6,16,1024]{3,2,1,0:T(8,128)(2,1)S(1)}, u32[]{:S(2)}, u32[]{:S(2)}) collective-permute-start(bf16[1,6,16,1024]{3,2,1,0:T(8,128)(2,1)S(1)} %get-tuple-element.194), channel_id=1, source_target_pairs={{0,64},{64,128},{128,192},{192,256},{256,320},{320,384},{384,448},... | collective-permute-start | bytes 589832 | tf_op jit(solution)/shard_map/while/body/eval_jaxpr/ppermute | solution.py:13
  192.1 11.5 %collective-permute-start = (bf16[1,6,16,1024]{3,2,1,0:T(8,128)(2,1)S(1)}, bf16[1,6,16,1024]{3,2,1,0:T(8,128)(2,1)S(1)}, u32[]{:S(2)}, u32[]{:S(2)}) collective-permute-start(bf16[1,6,16,1024]{3,2,1,0:T(8,128)(2,1)S(1)} %get-tuple-element.194), channel_id=1, source_target_pairs={{0,64},{64,128},{128,192},{192,256},{256,320},{320,384},{384,448},... | collective-permute-start | bytes 589832 | tf_op jit(solution)/shard_map/while/body/eval_jaxpr/ppermute | solution.py:13
  204.3 11.5 %collective-permute-start = (bf16[1,6,16,1024]{3,2,1,0:T(8,128)(2,1)S(1)}, bf16[1,6,16,1024]{3,2,1,0:T(8,128)(2,1)S(1)}, u32[]{:S(2)}, u32[]{:S(2)}) collective-permute-start(bf16[1,6,16,1024]{3,2,1,0:T(8,128)(2,1)S(1)} %get-tuple-element.194), channel_id=1, source_target_pairs={{0,64},{64,128},{128,192},{192,256},{256,320},{320,384},{384,448},... | collective-permute-start | bytes 589832 | tf_op jit(solution)/shard_map/while/body/eval_jaxpr/ppermute | solution.py:13
  216.5 11.5 %collective-permute-start = (bf16[1,6,16,1024]{3,2,1,0:T(8,128)(2,1)S(1)}, bf16[1,6,16,1024]{3,2,1,0:T(8,128)(2,1)S(1)}, u32[]{:S(2)}, u32[]{:S(2)}) collective-permute-start(bf16[1,6,16,1024]{3,2,1,0:T(8,128)(2,1)S(1)} %get-tuple-element.194), channel_id=1, source_target_pairs={{0,64},{64,128},{128,192},{192,256},{256,320},{320,384},{384,448},... | collective-permute-start | bytes 589832 | tf_op jit(solution)/shard_map/while/body/eval_jaxpr/ppermute | solution.py:13
  228.8 11.6 %collective-permute-start = (bf16[1,6,16,1024]{3,2,1,0:T(8,128)(2,1)S(1)}, bf16[1,6,16,1024]{3,2,1,0:T(8,128)(2,1)S(1)}, u32[]{:S(2)}, u32[]{:S(2)}) collective-permute-start(bf16[1,6,16,1024]{3,2,1,0:T(8,128)(2,1)S(1)} %get-tuple-element.194), channel_id=1, source_target_pairs={{0,64},{64,128},{128,192},{192,256},{256,320},{320,384},{384,448},... | collective-permute-start | bytes 589832 | tf_op jit(solution)/shard_map/while/body/eval_jaxpr/ppermute | solution.py:13
  241.1 12.7 %collective-permute-start = (bf16[1,6,16,1024]{3,2,1,0:T(8,128)(2,1)S(1)}, bf16[1,6,16,1024]{3,2,1,0:T(8,128)(2,1)S(1)}, u32[]{:S(2)}, u32[]{:S(2)}) collective-permute-start(bf16[1,6,16,1024]{3,2,1,0:T(8,128)(2,1)S(1)} %get-tuple-element.194), channel_id=1, source_target_pairs={{0,64},{64,128},{128,192},{192,256},{256,320},{320,384},{384,448},... | collective-permute-start | bytes 589832 | tf_op jit(solution)/shard_map/while/body/eval_jaxpr/ppermute | solution.py:13
  254.6 13.3 %collective-permute-start = (bf16[1,6,16,1024]{3,2,1,0:T(8,128)(2,1)S(1)}, bf16[1,6,16,1024]{3,2,1,0:T(8,128)(2,1)S(1)}, u32[]{:S(2)}, u32[]{:S(2)}) collective-permute-start(bf16[1,6,16,1024]{3,2,1,0:T(8,128)(2,1)S(1)} %get-tuple-element.194), channel_id=1, source_target_pairs={{0,64},{64,128},{128,192},{192,256},{256,320},{320,384},{384,448},... | collective-permute-start | bytes 589832 | tf_op jit(solution)/shard_map/while/body/eval_jaxpr/ppermute | solution.py:13
  268.7 12.4 %collective-permute-start = (bf16[1,6,16,1024]{3,2,1,0:T(8,128)(2,1)S(1)}, bf16[1,6,16,1024]{3,2,1,0:T(8,128)(2,1)S(1)}, u32[]{:S(2)}, u32[]{:S(2)}) collective-permute-start(bf16[1,6,16,1024]{3,2,1,0:T(8,128)(2,1)S(1)} %get-tuple-element.194), channel_id=1, source_target_pairs={{0,64},{64,128},{128,192},{192,256},{256,320},{320,384},{384,448},... | collective-permute-start | bytes 589832 | tf_op jit(solution)/shard_map/while/body/eval_jaxpr/ppermute | solution.py:13
  281.9 11.6 %collective-permute-start = (bf16[1,6,16,1024]{3,2,1,0:T(8,128)(2,1)S(1)}, bf16[1,6,16,1024]{3,2,1,0:T(8,128)(2,1)S(1)}, u32[]{:S(2)}, u32[]{:S(2)}) collective-permute-start(bf16[1,6,16,1024]{3,2,1,0:T(8,128)(2,1)S(1)} %get-tuple-element.194), channel_id=1, source_target_pairs={{0,64},{64,128},{128,192},{192,256},{256,320},{320,384},{384,448},... | collective-permute-start | bytes 589832 | tf_op jit(solution)/shard_map/while/body/eval_jaxpr/ppermute | solution.py:13
  294.2 11.5 %collective-permute-start = (bf16[1,6,16,1024]{3,2,1,0:T(8,128)(2,1)S(1)}, bf16[1,6,16,1024]{3,2,1,0:T(8,128)(2,1)S(1)}, u32[]{:S(2)}, u32[]{:S(2)}) collective-permute-start(bf16[1,6,16,1024]{3,2,1,0:T(8,128)(2,1)S(1)} %get-tuple-element.194), channel_id=1, source_target_pairs={{0,64},{64,128},{128,192},{192,256},{256,320},{320,384},{384,448},... | collective-permute-start | bytes 589832 | tf_op jit(solution)/shard_map/while/body/eval_jaxpr/ppermute | solution.py:13
  306.4 11.5 %collective-permute-start = (bf16[1,6,16,1024]{3,2,1,0:T(8,128)(2,1)S(1)}, bf16[1,6,16,1024]{3,2,1,0:T(8,128)(2,1)S(1)}, u32[]{:S(2)}, u32[]{:S(2)}) collective-permute-start(bf16[1,6,16,1024]{3,2,1,0:T(8,128)(2,1)S(1)} %get-tuple-element.194), channel_id=1, source_target_pairs={{0,64},{64,128},{128,192},{192,256},{256,320},{320,384},{384,448},... | collective-permute-start | bytes 589832 | tf_op jit(solution)/shard_map/while/body/eval_jaxpr/ppermute | solution.py:13
where the time goes:
time: 322 us; the launch traced here: 321 us
  waiting for transfers between devices  139 us (43%)
  blocking collectives  98.4 us (31%)
  starting transfers between devices  49.7 us (15%)
  local copies, waits for them, and re-layouts  15.5 us (5%)
  other arithmetic  15.5 us (5%)
    ppermute x15, waiting for transfers between devices, passed_along(): return lax.ppermute(value, axis, pairs)  139 us
    all_gather x1, blocking collectives, shards(): lax.all_gather(perturbation[0, :, :, last_cell], 'dom', axis=1, tiled=True)  98.4 us
    ppermute x15, starting transfers between devices, passed_along(): return lax.ppermute(value, axis, pairs)  30.3 us
    ppermute x1, starting transfers between devices, padded_2(): lax.ppermute(head, axis, [((i + 1) % count, i) for i in range(count)])  17.5 us
    add x15, other arithmetic, forward_step(): return (piece, total + table[step] * piece.astype(jnp.float32))  11 us
    dynamic_slice x15, local copies, waits for them, and re-layouts, forward_step(): return (piece, total + table[step] * piece.astype(jnp.float32))  9.17 us
  transfers between devices with their start and end apart: 17, of which 15 were waited for; matrix products, arithmetic and copies ran while one was open for 5% of the time, Pallas kernels for 0%

commit v1 on v0

v1 whole, which is shorter than its diff:
```python
import jax
import jax.numpy as jnp
import numpy as np
from jax import lax
from jax.sharding import Mesh, PartitionSpec as P

OMEGA = 0.5
NYQUIST = 2.0
INST = "inst"
DOM = ("ring", "far", "core")


def spectral_row(count):
    offs = jnp.arange(count, dtype=jnp.int32)
    sign = (1 - 2 * (offs % 2)).astype(jnp.float32)
    safe = jnp.maximum(offs, 1).astype(jnp.float32)
    angle = jnp.pi * safe / count
    cotan = jnp.where(offs == 0, 0.0, jnp.cos(angle) / jnp.sin(angle))
    return OMEGA * 0.5 * sign * cotan + NYQUIST * sign / count


def told_to_all(value, axis):
    count = lax.axis_size(axis)
    copies = jnp.broadcast_to(value[None], (count,) + value.shape)
    return lax.all_to_all(copies, axis, 0, 0, tiled=True)


def shards(perturbation, jacobian, flux_theta, flux_merid, donor_rows, donor_weights):
    count = lax.axis_size(INST)
    table = spectral_row(count)
    own = perturbation[0]
    nvar, rows, cells = own.shape
    lanes = cells // 8
    low = own.astype(jnp.bfloat16)
    blocks = low.reshape(2, nvar // 2, rows, 8, lanes).transpose(0, 3, 1, 2, 4)
    blocks = blocks.reshape(count, nvar // 2, rows, lanes)
    gathered = lax.all_to_all(blocks, INST, 0, 0, tiled=True)
    idx = jnp.arange(count, dtype=jnp.int32)
    matrix = table[(idx[:, None] - idx[None, :]) % count]
    mixed = jnp.einsum(
        "ij,jvtm->ivtm", matrix, gathered.astype(jnp.float32), precision=lax.Precision.HIGHEST
    )
    back = lax.all_to_all(mixed, INST, 0, 0, tiled=True)
    back = back.reshape(2, 8, nvar // 2, rows, lanes).transpose(0, 2, 3, 1, 4)
    temporal = back.reshape(nvar, rows, cells)
    temporal = temporal + table[0] * (own - low.astype(jnp.float32))

    ndom = lax.axis_size(DOM)
    before = lax.ppermute(own[:, -1:], DOM, [(i, (i + 1) % ndom) for i in range(ndom)])
    after = lax.ppermute(own[:, :1], DOM, [((i + 1) % ndom, i) for i in range(ndom)])
    padded = jnp.concatenate([before, own, after], axis=1)
    dtheta = padded[:, 2:] - padded[:, :-2]
    merid_pad = jnp.pad(own, ((0, 0), (0, 0), (1, 1)))
    dmerid = merid_pad[:, :, 2:] - merid_pad[:, :, :-2]
    spatial = jnp.sum(jacobian[0] * own[None], axis=1)
    for b in range(nvar):
        spatial = spatial + flux_theta[:, b, None, None] * dtheta[b][None]
        spatial = spatial + flux_merid[:, b, None, None] * dmerid[b][None]

    face = own[:, :, cells - 1]
    face = lax.all_gather(face, "core", axis=0)
    face = told_to_all(face, "far")
    face = told_to_all(face, "ring")
    outlet = face.transpose(3, 0, 1, 2, 4).reshape(nvar, ndom * rows)
    interp = jnp.zeros((nvar, rows), jnp.float32)
    for donor in range(2):
        picked = jnp.take(outlet, donor_rows[0, donor], axis=1)
        interp = interp + donor_weights[0, donor][None, :] * picked
    interface = own[:, :, 0] - interp
    product = temporal + spatial
    return product.at[:, :, 0].add(interface)[None]


def solution(mesh):
    inst = mesh.devices.shape[0]
    fine = Mesh(mesh.devices.reshape(inst, 8, 4, 2), (INST,) + DOM)
    in_specs = (
        P(INST, None, DOM, None),
        P(INST, None, None, DOM, None),
        P(),
        P(),
        P(INST, None, DOM),
        P(INST, None, DOM),
    )
    out_specs = P(INST, None, DOM, None)
    return jax.shard_map(shards, mesh=fine, in_specs=in_specs, out_specs=out_specs, check_vma=False)
```

time: 322 us -> 96.1 us (0.30)
  the two profiles are of different devices: /device:TPU:32 before, /device:TPU:2 now
where the time goes in v1:
time: 96.1 us; the launch traced here: 95.3 us
  starting transfers between devices  47.8 us (50%)
  waiting for transfers between devices  19.9 us (21%)
  local copies, waits for them, and re-layouts  16 us (17%)
  other arithmetic  9.06 us (9%)
  blocking collectives  1.79 us (2%)
    ppermute x1, starting transfers between devices, shards(): lax.ppermute(own[:, :1], DOM, [((i + 1) % ndom, i) for i in range(ndom)])  20.5 us
    all_to_all x2, waiting for transfers between devices, told_to_all(): return lax.all_to_all(copies, axis, 0, 0, tiled=True)  16.2 us
    all_to_all x2, starting transfers between devices, told_to_all(): return lax.all_to_all(copies, axis, 0, 0, tiled=True)  12.8 us
    all_to_all x1, starting transfers between devices, shards(): gathered = lax.all_to_all(blocks, INST, 0, 0, tiled=True)  7.58 us
    all_to_all x1, starting transfers between devices, shards(): back = lax.all_to_all(mixed, INST, 0, 0, tiled=True)  4.88 us
    all_to_all x1, waiting for transfers between devices, shards(): gathered = lax.all_to_all(blocks, INST, 0, 0, tiled=True)  2.64 us
    another operation x5, local copies, waits for them, and re-layouts  2.55 us
    reduce_sum x1, other arithmetic, shards(): spatial = jnp.sum(jacobian[0] * own[None], axis=1)  2.06 us
  transfers between devices with their start and end apart: 6, of which 4 were waited for; matrix products, arithmetic and copies ran while one was open for 21% of the time, Pallas kernels for 0%

profile of v1, /device:TPU:2, one launch (start us, length us, event | category | flops | bytes accessed | tf_op | source)
XLA Modules:
  0.0 95.3 jit_solution(15950086149739475179)
XLA Ops:
  0.0 1.1 %fusion.40 = (f32[6,1,1024]{2,1,0:T(1,128)S(1)}, f32[6,1,1024]{2,1,0:T(1,128)S(1)}) fusion(f32[6,16,1024]{2,1,0:T(8,128)} %bitcast.116), kind=kLoop, calls=%fused_computation.99 | loop fusion | bytes 98304 | tf_op jit(solution)/shard_map/slice | solution.py:50
  1.1 1.9 %collective-permute-start.1 = (f32[6,1,1024]{2,1,0:T(1,128)S(1)}, f32[6,1,1024]{2,1,0:T(1,128)S(1)}, u32[]{:S(2)}, u32[]{:S(2)}) collective-permute-start(f32[6,1,1024]{2,1,0:T(1,128)S(1)} %get-tuple-element.51), channel_id=1, source_target_pairs={{0,1},{1,2},{2,3},{3,4},{4,5},{5,6},{6,7},{7,8},{8,9},{9,10},{10,1... | collective-permute-start | bytes 73736 | tf_op jit(solution)/shard_map/ppermute | solution.py:49
  3.0 20.5 %collective-permute-start = (f32[6,1,1024]{2,1,0:T(1,128)S(1)}, f32[6,1,1024]{2,1,0:T(1,128)S(1)}, u32[]{:S(2)}, u32[]{:S(2)}) collective-permute-start(f32[6,1,1024]{2,1,0:T(1,128)S(1)} %get-tuple-element.50), channel_id=1, source_target_pairs={{1,0},{2,1},{3,2},{4,3},{5,4},{6,5},{7,6},{8,7},{9,8},{10,9},{11,1... | collective-permute-start | bytes 73736 | tf_op jit(solution)/shard_map/ppermute | solution.py:50
  23.6 0.9 fusion.39
  24.6 1.8 %all-gather = f32[12,16,1]{1,2,0:T(1,128)S(1)} all-gather(f32[6,16,1]{1,2,0:T(1,128)S(1)} %copy.60), channel_id=2, replica_groups=mesh['inst'=16,'ring'=8,'far'=4,'core'=2] {'core'}, dimensions={0}, use_global_device_ids=true | all-gather | bytes 1152 | tf_op jit(solution)/shard_map/all_gather | solution.py:61
  26.5 0.7 reshape.262
  27.2 5.7 %all-to-all-start.2 = ((f32[4,1,192]{2,1,0:T(1,128)}), f32[4,1,192]{2,1,0:T(1,128)S(1)}, u32[]{:S(2)}, u32[]{:S(2)}) async-start(f32[4,1,192]{2,1,0:T(1,128)} %reshape.262), calls=%async_computation.2 | async-start | bytes 8192 | tf_op jit(solution)/shard_map/all_to_all | solution.py:25
  32.9 2.1 %fusion = f32[6,16,1024]{2,1,0:T(8,128)S(1)} fusion(f32[1,6,6,16,1024]{4,3,2,1,0:T(8,128)} %param.11, f32[6,16,1024]{2,1,0:T(8,128)} %bitcast.118), kind=kLoop, calls=%fused_computation.4 | loop fusion | flops 1081344 | bytes 3145728 | tf_op jit(solution)/shard_map/reduce_sum | solution.py:55
  35.1 0.7 copy.56
  35.9 9.6 %all-to-all-done.2 = f32[4,1,192]{2,1,0:T(1,128)S(1)} async-done(((f32[4,1,192]{2,1,0:T(1,128)}), f32[4,1,192]{2,1,0:T(1,128)S(1)}, u32[]{:S(2)}, u32[]{:S(2)}) %all-to-all-start.2) | async-done | bytes 3104 | tf_op jit(solution)/shard_map/all_to_all | solution.py:25
  45.4 7.6 %all-to-all-start = ((bf16[16,3,16,128]{3,2,1,0:T(8,128)(2,1)}), bf16[16,3,16,128]{3,2,1,0:T(8,128)(2,1)S(1)}, u32[]{:S(2)}, u32[]{:S(2)}) async-start(bf16[16,3,16,128]{3,2,1,0:T(8,128)(2,1)} %bitcast.2), calls=%async_computation | async-start | bytes 393216 | tf_op jit(solution)/shard_map/all_to_all | solution.py:37
  53.1 1.9 %gather_fusion = f32[256]{0:T(256)S(1)} fusion(f32[16]{0:T(128)S(1)} %fusion.38, s32[1024]{0:T(1024)S(1)} %pad_clamp_fusion.2), kind=kCustom, calls=%fused_computation.2 | custom fusion | bytes 3072 | tf_op jit(solution)/shard_map/gather | solution.py:39
  55.0 0.6 slice_bitcast_fusion.13
  56.8 0.7 reduce.29
  57.7 0.8 reshape.264
  58.4 2.6 %all-to-all-done = bf16[16,3,16,128]{3,2,1,0:T(8,128)(2,1)S(1)} async-done(((bf16[16,3,16,128]{3,2,1,0:T(8,128)(2,1)}), bf16[16,3,16,128]{3,2,1,0:T(8,128)(2,1)S(1)}, u32[]{:S(2)}, u32[]{:S(2)}) %all-to-all-start) | async-done | bytes 196640 | tf_op jit(solution)/shard_map/all_to_all | solution.py:37
  61.1 7.1 %all-to-all-start.3 = ((f32[8,1,768]{2,1,0:T(1,128)}), f32[8,1,768]{2,1,0:T(1,128)S(1)}, u32[]{:S(2)}, u32[]{:S(2)}) async-start(f32[8,1,768]{2,1,0:T(1,128)} %reshape.264), calls=%async_computation.3 | async-start | bytes 49152 | tf_op jit(solution)/shard_map/all_to_all | solution.py:25
  68.5 0.9 copy.58
  69.4 6.6 %all-to-all-done.3 = f32[8,1,768]{2,1,0:T(1,128)S(1)} async-done(((f32[8,1,768]{2,1,0:T(1,128)}), f32[8,1,768]{2,1,0:T(1,128)S(1)}, u32[]{:S(2)}, u32[]{:S(2)}) %all-to-all-start.3) | async-done | bytes 24608 | tf_op jit(solution)/shard_map/all_to_all | solution.py:25
  76.0 4.9 %all-to-all-start.1 = ((f32[16,3,16,128]{3,2,1,0:T(8,128)}), f32[16,3,16,128]{3,2,1,0:T(8,128)S(1)}, u32[]{:S(2)}, u32[]{:S(2)}) async-start(f32[16,3,16,128]{3,2,1,0:T(8,128)} %copy.58), calls=%async_computation.1 | async-start | bytes 786432 | tf_op jit(solution)/shard_map/all_to_all | solution.py:43
  80.9 0.9 slice_reduce_fusion.11
  81.8 0.6 pad_clamp_fusion
  82.9 0.6 slice.198
  85.1 0.7 reduce.30
  86.6 0.7 gather_fusion.2
  87.4 0.7 gather_fusion.1
  88.2 0.7 fusion.31
  88.9 0.7 copy.66
  89.6 1.1 %all-to-all-done.1 = f32[16,3,16,128]{3,2,1,0:T(8,128)S(1)} async-done(((f32[16,3,16,128]{3,2,1,0:T(8,128)}), f32[16,3,16,128]{3,2,1,0:T(8,128)S(1)}, u32[]{:S(2)}, u32[]{:S(2)}) %all-to-all-start.1) | async-done | bytes 393248 | tf_op jit(solution)/shard_map/all_to_all | solution.py:43
  91.0 2.0 %fusion.14 = f32[1,6,16,1024]{3,2,1,0:T(8,128)} fusion(f32[6,16,1024]{2,1,0:T(8,128)S(1)} %fusion, f32[1,6,16,1024]{3,2,1,0:T(8,128)S(1)} %reshape.210, f32[1,6,16,1024]{3,2,1,0:T(8,128)S(1)} %copy-done, f32[16,1024]{1,0:T(8,128)S(1)} %get-tuple-element.43, f32[6]{0:T(128)} %get-tuple-element.28, f32[16,1024]{1,0:T(8,128)S(1)} %copy-done.4, ...), kind=kLoop, calls=%fused_computation.23 | loop fusion | flops 2949120 | bytes 2359588 | tf_op jit(solution)/shard_map/add | solution.py:70
  93.1 0.8 fusion.19
  93.9 1.4 %scatter-add.4 = f32[1,6,16,1024]{3,2,1,0:T(8,128)} dynamic-update-slice(f32[1,6,16,1024]{3,2,1,0:T(8,128)} %fusion.14, f32[1,6,16,1]{3,2,1,0:T(8,128)S(1)} %fusion.19, s32[]{:T(128)} %constant.79.clone.1, s32[]{:T(128)} %constant.79.clone.1, s32[]{:T(128)} %constant.79.clone.1, s32[]{:T(128)} %constant.79.clone.1) | dynamic-update-slice | bytes 772 | tf_op jit(solution)/shard_map/scatter-add | solution.py:71
  (79 shorter events, 5.2 us)
Async XLA Ops:
  0.0 35.1 %copy-start = (f32[1,6,16,1024]{3,2,1,0:T(8,128)S(1)}, f32[1,6,16,1024]{3,2,1,0:T(8,128)}, u32[]{:S(2)}) copy-start(f32[1,6,16,1024]{3,2,1,0:T(8,128)} %param.10) | copy-start | bytes 1179652
  1.1 81.3 %collective-permute-start.1 = (f32[6,1,1024]{2,1,0:T(1,128)S(1)}, f32[6,1,1024]{2,1,0:T(1,128)S(1)}, u32[]{:S(2)}, u32[]{:S(2)}) collective-permute-start(f32[6,1,1024]{2,1,0:T(1,128)S(1)} %get-tuple-element.51), channel_id=1, source_target_pairs={{0,1},{1,2},{2,3},{3,4},{4,5},{5,6},{6,7},{7,8},{8,9},{9,10},{10,1... | collective-permute-start | bytes 73736 | tf_op jit(solution)/shard_map/ppermute | solution.py:49
  3.0 79.4 %collective-permute-start = (f32[6,1,1024]{2,1,0:T(1,128)S(1)}, f32[6,1,1024]{2,1,0:T(1,128)S(1)}, u32[]{:S(2)}, u32[]{:S(2)}) collective-permute-start(f32[6,1,1024]{2,1,0:T(1,128)S(1)} %get-tuple-element.50), channel_id=1, source_target_pairs={{1,0},{2,1},{3,2},{4,3},{5,4},{6,5},{7,6},{8,7},{9,8},{10,9},{11,1... | collective-permute-start | bytes 73736 | tf_op jit(solution)/shard_map/ppermute | solution.py:50
  27.2 18.2 %all-to-all-start.2 = ((f32[4,1,192]{2,1,0:T(1,128)}), f32[4,1,192]{2,1,0:T(1,128)S(1)}, u32[]{:S(2)}, u32[]{:S(2)}) async-start(f32[4,1,192]{2,1,0:T(1,128)} %reshape.262), calls=%async_computation.2 | async-start | bytes 8192 | tf_op jit(solution)/shard_map/all_to_all | solution.py:25
  45.4 15.7 %all-to-all-start = ((bf16[16,3,16,128]{3,2,1,0:T(8,128)(2,1)}), bf16[16,3,16,128]{3,2,1,0:T(8,128)(2,1)S(1)}, u32[]{:S(2)}, u32[]{:S(2)}) async-start(bf16[16,3,16,128]{3,2,1,0:T(8,128)(2,1)} %bitcast.2), calls=%async_computation | async-start | bytes 393216 | tf_op jit(solution)/shard_map/all_to_all | solution.py:37
  53.0 2.0 %copy-start.21 = (f32[1,2,16]{2,1,0:T(2,128)S(1)}, f32[1,2,16]{2,1,0:T(2,128)}, u32[]{:S(2)}) copy-start(f32[1,2,16]{2,1,0:T(2,128)} %param.15) | copy-start | bytes 388
  53.1 2.6 %copy-start.20 = (s32[1,2,16]{2,1,0:T(2,128)S(1)}, s32[1,2,16]{2,1,0:T(2,128)}, u32[]{:S(2)}) copy-start(s32[1,2,16]{2,1,0:T(2,128)} %param.14) | copy-start | bytes 388
  54.9 26.0 %copy-start.6 = (f32[6,6]{1,0:T(8,128)S(1)}, f32[6,6]{1,0:T(8,128)}, u32[]{:S(2)}) copy-start(f32[6,6]{1,0:T(8,128)} %param.13) | copy-start | bytes 436
  55.0 25.9 %copy-start.7 = (f32[6,6]{1,0:T(8,128)S(1)}, f32[6,6]{1,0:T(8,128)}, u32[]{:S(2)}) copy-start(f32[6,6]{1,0:T(8,128)} %param.12) | copy-start | bytes 436
  61.1 14.9 %all-to-all-start.3 = ((f32[8,1,768]{2,1,0:T(1,128)}), f32[8,1,768]{2,1,0:T(1,128)S(1)}, u32[]{:S(2)}, u32[]{:S(2)}) async-start(f32[8,1,768]{2,1,0:T(1,128)} %reshape.264), calls=%async_computation.3 | async-start | bytes 49152 | tf_op jit(solution)/shard_map/all_to_all | solution.py:25
  76.0 14.7 %all-to-all-start.1 = ((f32[16,3,16,128]{3,2,1,0:T(8,128)}), f32[16,3,16,128]{3,2,1,0:T(8,128)S(1)}, u32[]{:S(2)}, u32[]{:S(2)}) async-start(f32[16,3,16,128]{3,2,1,0:T(8,128)} %copy.58), calls=%async_computation.1 | async-start | bytes 786432 | tf_op jit(solution)/shard_map/all_to_all | solution.py:43
  81.8 4.3 %copy-start.12 = (f32[6]{0:T(128)}, f32[6]{0:T(128)S(1)}, u32[]{:S(2)}) copy-start(f32[6]{0:T(128)S(1)} %get-tuple-element.24) | copy-start | bytes 76
  81.8 4.3 %copy-start.13 = (f32[6]{0:T(128)}, f32[6]{0:T(128)S(1)}, u32[]{:S(2)}) copy-start(f32[6]{0:T(128)S(1)} %get-tuple-element.26) | copy-start | bytes 76
  81.8 4.3 %copy-start.14 = (f32[6]{0:T(128)}, f32[6]{0:T(128)S(1)}, u32[]{:S(2)}) copy-start(f32[6]{0:T(128)S(1)} %get-tuple-element.27) | copy-start | bytes 76
  81.8 4.3 %copy-start.15 = (f32[6]{0:T(128)}, f32[6]{0:T(128)S(1)}, u32[]{:S(2)}) copy-start(f32[6]{0:T(128)S(1)} %get-tuple-element.64) | copy-start | bytes 76
  81.8 4.3 %copy-start.16 = (f32[6]{0:T(128)}, f32[6]{0:T(128)S(1)}, u32[]{:S(2)}) copy-start(f32[6]{0:T(128)S(1)} %get-tuple-element.65) | copy-start | bytes 76
  81.8 4.3 %copy-start.17 = (f32[6]{0:T(128)}, f32[6]{0:T(128)S(1)}, u32[]{:S(2)}) copy-start(f32[6]{0:T(128)S(1)} %get-tuple-element.66) | copy-start | bytes 76
  81.8 4.3 %copy-start.18 = (f32[6]{0:T(128)}, f32[6]{0:T(128)S(1)}, u32[]{:S(2)}) copy-start(f32[6]{0:T(128)S(1)} %get-tuple-element.67) | copy-start | bytes 76
  81.8 4.3 %copy-start.19 = (f32[6]{0:T(128)}, f32[6]{0:T(128)S(1)}, u32[]{:S(2)}) copy-start(f32[6]{0:T(128)S(1)} %get-tuple-element.25) | copy-start | bytes 76
  82.8 3.3 %copy-start.1 = (f32[16,1024]{1,0:T(8,128)}, f32[16,1024]{1,0:T(8,128)S(1)}, u32[]{:S(2)}) copy-start(f32[16,1024]{1,0:T(8,128)S(1)} %get-tuple-element.59) | copy-start | bytes 196612
  82.8 3.3 %copy-start.3 = (f32[16,1024]{1,0:T(8,128)}, f32[16,1024]{1,0:T(8,128)S(1)}, u32[]{:S(2)}) copy-start(f32[16,1024]{1,0:T(8,128)S(1)} %get-tuple-element.60) | copy-start | bytes 196612
  88.1 2.9 %copy-start.2 = (f32[16,1024]{1,0:T(8,128)S(1)}, f32[16,1024]{1,0:T(8,128)}, u32[]{:S(2)}) copy-start(f32[16,1024]{1,0:T(8,128)} %copy-done.1) | copy-start | bytes 196612
  88.1 2.9 %copy-start.4 = (f32[16,1024]{1,0:T(8,128)S(1)}, f32[16,1024]{1,0:T(8,128)}, u32[]{:S(2)}) copy-start(f32[16,1024]{1,0:T(8,128)} %copy-done.3) | copy-start | bytes 196612
  90.7 2.4 %copy-start.11 = (f32[6]{0:T(128)S(1)}, f32[6]{0:T(128)}, u32[]{:S(2)}) copy-start(f32[6]{0:T(128)} %get-tuple-element.28) | copy-start | bytes 76
  90.9 2.1 %copy-start.5 = (f32[6,16,1]{2,1,0:T(8,128)S(1)}, f32[6,16,1]{2,1,0:T(8,128)}, u32[]{:S(2)}) copy-start(f32[6,16,1]{2,1,0:T(8,128)} %copy.66) | copy-start | bytes 1156
  91.0 2.1 %copy-start.8 = (f32[16,1]{1,0:T(8,128)S(1)}, f32[16,1]{1,0:T(8,128)}, u32[]{:S(2)}) copy-start(f32[16,1]{1,0:T(8,128)} %slice.198) | copy-start | bytes 196
  91.0 2.1 %copy-start.9 = (f32[16,1]{1,0:T(8,128)S(1)}, f32[16,1]{1,0:T(8,128)}, u32[]{:S(2)}) copy-start(f32[16,1]{1,0:T(8,128)} %slice.197) | copy-start | bytes 196
  91.0 2.1 %copy-start.10 = (f32[16,1]{1,0:T(8,128)S(1)}, f32[16,1]{1,0:T(8,128)}, u32[]{:S(2)}) copy-start(f32[16,1]{1,0:T(8,128)} %slice.196) | copy-start | bytes 196

commit v2 on v1

v2 whole, which is shorter than its diff:
```python
import functools
import math

import jax
import jax.numpy as jnp
from jax import lax
from jax.experimental import pallas as pl
from jax.experimental.pallas import tpu as pltpu
from jax.sharding import Mesh, PartitionSpec as P

OMEGA = 0.5
NYQUIST = 2.0
INST = "inst"
RING, FAR, CORE = "ring", "far", "core"
DOM = (RING, FAR, CORE)
LANES = 128
F32 = jnp.float32
VMEM_BYTES = 12 * 2**20


def whole(count):
    return [pl.BlockSpec(memory_space=pltpu.VMEM) for _ in range(count)]


def call(body, operands, specs, outs, flops, name, scratch=()):
    moved = sum(math.prod(v.shape) * v.dtype.itemsize for v in list(operands) + list(outs))
    return pl.pallas_call(
        body,
        out_shape=outs,
        in_specs=specs,
        out_specs=whole(len(outs)),
        scratch_shapes=scratch,
        compiler_params=pltpu.CompilerParams(vmem_limit_bytes=VMEM_BYTES),
        cost_estimate=pl.CostEstimate(flops=flops, bytes_accessed=moved, transcendentals=0),
        name=name,
    )(*operands)


def antisymmetric(count):
    return [OMEGA * 0.5 * (-1) ** k / math.tan(math.pi * k / count) for k in range(1, count // 2)]


def prepare(p_ref, blocks_ref, face_ref, sibling_ref, outer_ref):
    nvar, rows, cells = p_ref.shape[1:]
    chunks = cells // LANES
    upper = lax.axis_index(CORE) == 1
    low = p_ref[0].astype(jnp.bfloat16)
    third = nvar // 2
    for h in range(2):
        for c in range(chunks):
            blocks_ref[h * chunks + c] = low[h * third : (h + 1) * third, :, c * LANES : (c + 1) * LANES]
    lane = lax.broadcasted_iota(jnp.int32, (rows, LANES), 1)
    line = lax.broadcasted_iota(jnp.int32, (rows, LANES), 0)
    picked = jnp.zeros((rows, LANES), F32)
    for v in range(nvar):
        last = jnp.broadcast_to(p_ref[0, v, :, cells - 1 : cells], (rows, LANES))
        picked = jnp.where(lane == v * rows + line, last, picked)
    face = jnp.sum(picked, axis=0, keepdims=True)
    face_ref[...] = jnp.broadcast_to(face[None], face_ref.shape)
    first, final = p_ref[0, :, 0, :], p_ref[0, :, rows - 1, :]
    sibling_ref[...] = jnp.where(upper, first, final)
    outer_ref[...] = jnp.where(upper, final, first)


def mix(got_ref, near_ref, mixed_ref, told_ref):
    count, third = got_ref.shape[0], got_ref.shape[1]
    half = count // 2
    deriv = antisymmetric(count)
    for v in range(third):
        a = [got_ref[j, v].astype(F32) for j in range(count)]
        even, odd = a[0], a[1]
        for j in range(2, count, 2):
            even, odd = even + a[j], odd + a[j + 1]
        filt = (even - odd) * (NYQUIST / count)
        for i in range(half):
            gap = [a[(i - k) % count] - a[(i + k) % count] for k in range(1, half)]
            here, there = deriv[0] * gap[0], deriv[half - 2] * gap[0]
            for k in range(1, half - 1):
                here, there = here + deriv[k] * gap[k], there + deriv[half - 2 - k] * gap[k]
            sign = filt if i % 2 == 0 else -filt
            mixed_ref[i, v] = here + sign
            mixed_ref[i + half, v] = (sign if half % 2 == 0 else -sign) - there
    told_ref[...] = jnp.broadcast_to(near_ref[:, 0, :][None], told_ref.shape)


def space(count, p_ref, jac_ref, theta_ref, merid_ref, pair_ref, outer_ref, out_ref, dm_ref):
    nvar, rows, cells = p_ref.shape[1:]
    core = lax.axis_index(CORE)
    upper = core == 1
    lane = lax.broadcasted_iota(jnp.int32, (rows, cells), 1)
    line = lax.broadcasted_iota(jnp.int32, (rows, LANES), 0)
    for b in range(nvar):
        x = p_ref[0, b]
        right = jnp.where(lane == cells - 1, 0.0, pltpu.roll(x, cells - 1, 1))
        left = jnp.where(lane == 0, 0.0, pltpu.roll(x, 1, 1))
        dm_ref[b] = right - left
    for c in range(cells // LANES):
        part = slice(c * LANES, (c + 1) * LANES)
        sibling = pair_ref[1 - core, :, part]
        outer = outer_ref[:, part]
        before = jnp.where(upper, sibling, outer)
        after = jnp.where(upper, outer, sibling)
        xs, ths, dms = [], [], []
        for b in range(nvar):
            x = p_ref[0, b, :, part]
            up = jnp.where(line == rows - 1, after[b : b + 1], pltpu.roll(x, rows - 1, 0))
            down = jnp.where(line == 0, before[b : b + 1], pltpu.roll(x, 1, 0))
            xs.append(x)
            ths.append(up - down)
            dms.append(dm_ref[b, :, part])
        for a in range(nvar):
            acc = (xs[a] - xs[a].astype(jnp.bfloat16).astype(F32)) * (NYQUIST / count)
            for b in range(nvar):
                acc = acc + jac_ref[0, a, b, :, part] * xs[b]
                acc = acc + theta_ref[a, b] * ths[b]
                acc = acc + merid_ref[a, b] * dms[b]
            out_ref[a, :, part] = acc


def finish(sum_ref, back_ref, faces_ref, p_ref, weights_ref, rows_ref, out_ref, got_ref):
    nvar, rows, cells = sum_ref.shape
    chunks = cells // LANES
    third = nvar // 2
    for h in range(2):
        for c in range(chunks):
            part = slice(c * LANES, (c + 1) * LANES)
            own = slice(h * third, (h + 1) * third)
            out_ref[0, own, :, part] = sum_ref[own, :, part] + back_ref[h * chunks + c]
    lane = lax.broadcasted_iota(jnp.int32, (rows, LANES), 1)
    line = lax.broadcasted_iota(jnp.int32, (rows, LANES), 0)
    total = jnp.zeros((rows, LANES), F32)
    for donor in range(2):
        within = jnp.zeros((rows, LANES), jnp.int32)
        for t in range(rows):
            r = rows_ref[0, donor, t]
            device, spot = r // rows, r % rows
            got_ref[donor, t : t + 1, :] = faces_ref[device // 8, pl.ds(device % 8, 1), :]
            within = jnp.where(line == t, spot, within)
        weight = jnp.broadcast_to(weights_ref[0, donor : donor + 1, :], (rows, rows))
        square = (rows, rows)
        eye = lax.broadcasted_iota(jnp.int32, square, 0) == lax.broadcasted_iota(jnp.int32, square, 1)
        weight = jnp.sum(jnp.where(eye, weight, 0.0), axis=1, keepdims=True)
        total = total + jnp.where(lane % rows == within, got_ref[donor], 0.0) * weight
    for v in range(nvar):
        mine = jnp.where(lane // rows == v, total, 0.0)
        interp = jnp.sum(mine, axis=1, keepdims=True)
        head = out_ref[0, v, :, :LANES]
        interface = p_ref[0, v, :, :LANES] - interp
        out_ref[0, v, :, :LANES] = head + jnp.where(lane == 0, interface, 0.0)


def shards(perturbation, jacobian, flux_theta, flux_merid, donor_rows, donor_weights):
    count, far, ring = lax.axis_size(INST), lax.axis_size(FAR), lax.axis_size(RING)
    ndom = lax.axis_size(DOM)
    _, nvar, rows, cells = perturbation.shape
    smem = pl.BlockSpec(memory_space=pltpu.SMEM)
    blocks, face, sibling, outer = call(
        prepare,
        (perturbation,),
        whole(1),
        (
            jax.ShapeDtypeStruct((count, nvar // 2, rows, LANES), jnp.bfloat16),
            jax.ShapeDtypeStruct((far * 2, 8, LANES), F32),
            jax.ShapeDtypeStruct((nvar, cells), F32),
            jax.ShapeDtypeStruct((nvar, cells), F32),
        ),
        10**6,
        "prepare",
    )
    swaps = [(c, (c + (1 if c % 2 else -1)) % ndom) for c in range(ndom)]
    outer = lax.ppermute(outer, DOM, swaps)
    near = lax.all_to_all(face, (FAR, CORE), 0, 0, tiled=True)
    got = lax.all_to_all(blocks, INST, 0, 0, tiled=True)
    pair = lax.all_gather(sibling, CORE, axis=0)
    total = call(
        functools.partial(space, count),
        (perturbation, jacobian, flux_theta, flux_merid, pair, outer),
        whole(2) + [smem, smem] + whole(2),
        (jax.ShapeDtypeStruct((nvar, rows, cells), F32),),
        2 * 18 * nvar * rows * cells,
        "space",
        [pltpu.VMEM((nvar, rows, cells), F32)],
    )[0]
    mixed, told = call(
        mix,
        (got, near),
        whole(2),
        (
            jax.ShapeDtypeStruct((count, nvar // 2, rows, LANES), F32),
            jax.ShapeDtypeStruct((ring, far * 2, LANES), F32),
        ),
        2 * 16 * nvar * rows * cells,
        "mix",
    )
    back = lax.all_to_all(mixed, INST, 0, 0, tiled=True)
    faces = lax.all_to_all(told, RING, 0, 0, tiled=True)
    return call(
        finish,
        (total, back, faces, perturbation, donor_weights, donor_rows),
        whole(5) + [smem],
        (jax.ShapeDtypeStruct(perturbation.shape, F32),),
        3 * nvar * rows * cells,
        "finish",
        [pltpu.VMEM((2, rows, LANES), F32)],
    )[0]


def solution(mesh):
    inst = mesh.devices.shape[0]
    fine = Mesh(mesh.devices.reshape(inst, 8, 4, 2), (INST,) + DOM)
    in_specs = (
        P(INST, None, DOM, None),
        P(INST, None, None, DOM, None),
        P(),
        P(),
        P(INST, None, DOM),
        P(INST, None, DOM),
    )
    out_specs = P(INST, None, DOM, None)
    return jax.shard_map(shards, mesh=fine, in_specs=in_specs, out_specs=out_specs, check_vma=False)
```

time: 96.1 us -> 87.9 us (0.915)
  blocking collectives: 1.79 us -> 64.2 us
  starting transfers between devices: 47.8 us -> 6.74 us
  waiting for transfers between devices: 19.9 us -> 7.14 us
  local copies, waits for them, and re-layouts: 16 us -> 5.04 us
  other arithmetic: 9.06 us -> 0 us
  Pallas kernels: 0 us -> 4.25 us
    all_to_all x0 -> x3, blocking collectives: none -> 61.9 us  [the longest x1 31.9 us: shards(): near = lax.all_to_all(face, (FAR, CORE), 0, 0, tiled=True)]
    ppermute x2 -> x1, starting transfers between devices: 22.5 us -> 1.91 us  [shards(): outer = lax.ppermute(outer, DOM, swaps)]
    all_to_all x3 -> x0, starting transfers between devices: 20.4 us -> none  [the longest x2 12.8 us: told_to_all(): return lax.all_to_all(copies, axis, 0, 0, tiled=True)]
    all_to_all x3 -> x0, waiting for transfers between devices: 18.8 us -> none  [the longest x2 16.2 us: told_to_all(): return lax.all_to_all(copies, axis, 0, 0, tiled=True)]
    ppermute x2 -> x1, waiting for transfers between devices: 0.01 us -> 7.14 us  [shards(): outer = lax.ppermute(outer, DOM, swaps)]
    pallas_call x0 -> x4, Pallas kernels: none -> 4.25 us  [call(): pl.pallas_call(body, out_shape=outs, in_specs=specs, out_specs=whole(len(...]
    gather x6 -> x0, local copies, waits for them, and re-layouts: 3.47 us -> none  [the longest x2 1.94 us: shards(): matrix = table[(idx[:, None] - idx[None, :]) % count]]
    unnamed x51 -> x16, local copies, waits for them, and re-layouts: 1.9 us -> 5.04 us
  transfers between devices with their start and end apart: 6 -> 2, of which waited for: 4 -> 1; matrix products, arithmetic and copies ran while one was open for 21% -> 0% of each run, Pallas kernels for 0% -> 2%
where the time goes in v2:
time: 87.9 us; the launch traced here: 87.4 us
  blocking collectives  64.2 us (73%)
  waiting for transfers between devices  7.14 us (8%)
  starting transfers between devices  6.74 us (8%)
  local copies, waits for them, and re-layouts  5.04 us (6%)
  Pallas kernels  4.25 us (5%)
    all_to_all x1, blocking collectives, shards(): near = lax.all_to_all(face, (FAR, CORE), 0, 0, tiled=True)  31.9 us
    all_to_all x1, blocking collectives, shards(): got = lax.all_to_all(blocks, INST, 0, 0, tiled=True)  15.1 us
    all_to_all x1, blocking collectives, shards(): faces = lax.all_to_all(told, RING, 0, 0, tiled=True)  14.9 us
    ppermute x1, waiting for transfers between devices, shards(): outer = lax.ppermute(outer, DOM, swaps)  7.14 us
    unnamed x16, local copies, waits for them, and re-layouts  5.04 us
    all_to_all x1, starting transfers between devices, shards(): back = lax.all_to_all(mixed, INST, 0, 0, tiled=True)  4.83 us
    pallas_call x4, Pallas kernels, call(): pl.pallas_call(body, out_shape=outs, in_specs=specs, out_specs=whole(len(...  4.25 us
    all_gather x1, blocking collectives, shards(): pair = lax.all_gather(sibling, CORE, axis=0)  2.29 us
  transfers between devices with their start and end apart: 2, of which 1 were waited for; matrix products, arithmetic and copies ran while one was open for 0% of the time, Pallas kernels for 2%

profile of v2, /device:TPU:2, one launch (start us, length us, event | category | flops | bytes accessed | tf_op | source)
XLA Modules:
  0.0 87.4 jit_solution(14503685012588648581)
XLA Ops:
  0.0 0.0 copy-start
  0.0 1.0 %copy-done = f32[1,6,16,1024]{3,2,1,0:T(8,128)S(1)} copy-done((f32[1,6,16,1024]{3,2,1,0:T(8,128)S(1)}, f32[1,6,16,1024]{3,2,1,0:T(8,128)}, u32[]{:S(2)}) %copy-start) | copy-done | bytes 393240
  1.0 0.1 prepare.1
  1.1 31.9 %all_to_all.20.near_ref = f32[8,8,128]{2,1,0:T(8,128)S(1)} all-to-all(f32[8,8,128]{2,1,0:T(8,128)S(1)} %get-tuple-element.14), channel_id=1, replica_groups=mesh['inst'=16,'ring'=8,'far'=4,'core'=2] {'far','core'}, dimensions={0} | all-to-all | bytes 65536 | tf_op jit(solution)/shard_map/all_to_all | solution.py:172
  32.9 0.0 copy-start.2
  32.9 0.0 copy-start.6
  32.9 0.0 copy-start.7
  33.0 15.1 %all_to_all.21.got_ref = bf16[16,3,16,128]{3,2,1,0:T(8,128)(2,1)S(1)} all-to-all(bf16[16,3,16,128]{3,2,1,0:T(8,128)(2,1)S(1)} %get-tuple-element.13), channel_id=1, replica_groups=mesh['inst'=16,'ring'=8,'far'=4,'core'=2] {'inst'}, dimensions={0} | all-to-all | bytes 393216 | tf_op jit(solution)/shard_map/all_to_all | solution.py:173
  48.1 1.0 %mix.1 = (f32[16,3,16,128]{3,2,1,0:T(8,128)}, f32[8,8,128]{2,1,0:T(8,128)S(1)}) custom-call(bf16[16,3,16,128]{3,2,1,0:T(8,128)(2,1)S(1)} %all_to_all.21.got_ref, f32[8,8,128]{2,1,0:T(8,128)S(1)} %all_to_all.20.near_ref), custom_call_target="tpu_custom_call" | custom-call | flops 3145728 | bytes 655360 | tf_op jit(solution)/shard_map/mix/pallas_call | solution.py:27
  49.0 14.9 %all_to_all.22.faces_ref = f32[8,8,128]{2,1,0:T(8,128)S(1)} all-to-all(f32[8,8,128]{2,1,0:T(8,128)S(1)} %get-tuple-element.16), channel_id=1, replica_groups=mesh['inst'=16,'ring'=8,'far'=4,'core'=2] {'ring'}, dimensions={0} | all-to-all | bytes 65536 | tf_op jit(solution)/shard_map/all_to_all | solution.py:196
  64.0 4.8 %all-to-all-start.2 = ((f32[16,3,16,128]{3,2,1,0:T(8,128)}), f32[16,3,16,128]{3,2,1,0:T(8,128)S(1)}, u32[]{:S(2)}, u32[]{:S(2)}) async-start(f32[16,3,16,128]{3,2,1,0:T(8,128)} %get-tuple-element.15), calls=%async_computation.2 | async-start | bytes 786432 | tf_op jit(solution)/shard_map/all_to_all | solution.py:195
  68.8 1.9 %collective-permute-start = (f32[6,1024]{1,0:T(8,128)S(1)}, f32[6,1024]{1,0:T(8,128)S(1)}, u32[]{:S(2)}, u32[]{:S(2)}) collective-permute-start(f32[6,1024]{1,0:T(8,128)S(1)} %get-tuple-element.12), channel_id=1, source_target_pairs={{0,63},{1,2},{2,1},{3,4},{4,3},{5,6},{6,5},{7,8},{8,7},{9,10},{10,... | collective-permute-start | bytes 73736 | tf_op jit(solution)/shard_map/ppermute | solution.py:171
  70.7 2.3 %all-gather.1.pair_ref = f32[2,6,1024]{2,1,0:T(8,128)S(1)} all-gather(f32[1,6,1024]{2,1,0:T(8,128)S(1)} %bitcast.1), channel_id=2, replica_groups=mesh['inst'=16,'ring'=8,'far'=4,'core'=2] {'core'}, dimensions={0}, use_global_device_ids=true | all-gather | bytes 73728 | tf_op jit(solution)/shard_map/all_gather | solution.py:174
  73.0 7.1 %collective-permute-done.outer_ref = f32[6,1024]{1,0:T(8,128)S(1)} collective-permute-done((f32[6,1024]{1,0:T(8,128)S(1)}, f32[6,1024]{1,0:T(8,128)S(1)}, u32[]{:S(2)}, u32[]{:S(2)}) %collective-permute-start) | collective-permute-done | bytes 24608 | tf_op jit(solution)/shard_map/ppermute | solution.py:171
  80.1 0.0 copy-start.1
  80.1 1.0 %copy-done.1 = f32[1,6,16,1024]{3,2,1,0:T(8,128)S(1)} copy-done((f32[1,6,16,1024]{3,2,1,0:T(8,128)S(1)}, f32[1,6,16,1024]{3,2,1,0:T(8,128)}, u32[]{:S(2)}) %copy-start.1) | copy-done | bytes 393240
  81.1 0.0 copy-start.3
  81.1 1.7 %copy-done.3 = f32[1,6,6,16,1024]{4,3,2,1,0:T(8,128)S(1)} copy-done((f32[1,6,6,16,1024]{4,3,2,1,0:T(8,128)S(1)}, f32[1,6,6,16,1024]{4,3,2,1,0:T(8,128)}, u32[]{:S(2)}) %copy-start.3) | copy-done | bytes 2359320
  82.8 0.0 copy-start.4
  82.8 0.7 copy-done.4
  83.5 0.0 copy-start.5
  83.5 0.7 copy-done.5
  84.2 1.4 %space.1.sum_ref = f32[6,16,1024]{2,1,0:T(8,128)S(1)} custom-call(f32[1,6,16,1024]{3,2,1,0:T(8,128)S(1)} %copy-done.1, f32[1,6,6,16,1024]{4,3,2,1,0:T(8,128)S(1)} %copy-done.3, f32[6,6]{1,0:T(8,128)S(1)} %copy-done.4, f32[6,6]{1,0:T(8,128)S(1)} %copy-done.5, f32[2,6,1024]{2,1,0:T(8,128)S(1)} %all-gather.1.pair_ref, f32[6,1024]{1,0:T(8,128)S(1)} %collective-permute-done.outer_ref), custom_call_target="tpu_custom_call" | custom-call | flops 3538944 | bytes 3219744 | tf_op jit(solution)/shard_map/space/pallas_call | solution.py:27
  85.6 0.0 all-to-all-done.2.back_ref
  85.6 0.0 copy-done.2
  85.6 0.0 copy-done.6
  85.6 0.0 copy-done.7
  85.6 1.8 %finish.1 = f32[1,6,16,1024]{3,2,1,0:T(8,128)} custom-call(f32[6,16,1024]{2,1,0:T(8,128)S(1)} %space.1.sum_ref, f32[16,3,16,128]{3,2,1,0:T(8,128)S(1)} %all-to-all-done.2.back_ref, f32[8,8,128]{2,1,0:T(8,128)S(1)} %all_to_all.22.faces_ref, f32[1,6,16,1024]{3,2,1,0:T(8,128)S(1)} %copy-done.2, f32[1,2,16]{2,1,0:T(2,128)S(1)} %copy-done.6, ...), custom_call_target="tpu_custom_call" | custom-call | flops 294912 | bytes 1605888 | tf_op jit(solution)/shard_map/finish/pallas_call | solution.py:27
Async XLA Ops:
  0.0 1.0 %copy-start = (f32[1,6,16,1024]{3,2,1,0:T(8,128)S(1)}, f32[1,6,16,1024]{3,2,1,0:T(8,128)}, u32[]{:S(2)}) copy-start(f32[1,6,16,1024]{3,2,1,0:T(8,128)} %p_ref.5) | copy-start | bytes 1179652
  32.9 52.7 %copy-start.2 = (f32[1,6,16,1024]{3,2,1,0:T(8,128)S(1)}, f32[1,6,16,1024]{3,2,1,0:T(8,128)}, u32[]{:S(2)}) copy-start(f32[1,6,16,1024]{3,2,1,0:T(8,128)} %p_ref.5) | copy-start | bytes 1179652
  32.9 52.7 %copy-start.6 = (f32[1,2,16]{2,1,0:T(2,128)S(1)}, f32[1,2,16]{2,1,0:T(2,128)}, u32[]{:S(2)}) copy-start(f32[1,2,16]{2,1,0:T(2,128)} %weights_ref.1) | copy-start | bytes 388
  32.9 52.7 %copy-start.7 = (s32[1,2,16]{2,1,0:T(2,128)S(1)}, s32[1,2,16]{2,1,0:T(2,128)}, u32[]{:S(2)}) copy-start(s32[1,2,16]{2,1,0:T(2,128)} %rows_ref.1) | copy-start | bytes 388
  64.0 21.6 %all-to-all-start.2 = ((f32[16,3,16,128]{3,2,1,0:T(8,128)}), f32[16,3,16,128]{3,2,1,0:T(8,128)S(1)}, u32[]{:S(2)}, u32[]{:S(2)}) async-start(f32[16,3,16,128]{3,2,1,0:T(8,128)} %get-tuple-element.15), calls=%async_computation.2 | async-start | bytes 786432 | tf_op jit(solution)/shard_map/all_to_all | solution.py:195
  68.8 11.3 %collective-permute-start = (f32[6,1024]{1,0:T(8,128)S(1)}, f32[6,1024]{1,0:T(8,128)S(1)}, u32[]{:S(2)}, u32[]{:S(2)}) collective-permute-start(f32[6,1024]{1,0:T(8,128)S(1)} %get-tuple-element.12), channel_id=1, source_target_pairs={{0,63},{1,2},{2,1},{3,4},{4,3},{5,6},{6,5},{7,8},{8,7},{9,10},{10,... | collective-permute-start | bytes 73736 | tf_op jit(solution)/shard_map/ppermute | solution.py:171
  80.1 1.0 %copy-start.1 = (f32[1,6,16,1024]{3,2,1,0:T(8,128)S(1)}, f32[1,6,16,1024]{3,2,1,0:T(8,128)}, u32[]{:S(2)}) copy-start(f32[1,6,16,1024]{3,2,1,0:T(8,128)} %p_ref.5) | copy-start | bytes 1179652
  81.1 1.7 %copy-start.3 = (f32[1,6,6,16,1024]{4,3,2,1,0:T(8,128)S(1)}, f32[1,6,6,16,1024]{4,3,2,1,0:T(8,128)}, u32[]{:S(2)}) copy-start(f32[1,6,6,16,1024]{4,3,2,1,0:T(8,128)} %jac_ref.1) | copy-start | bytes 7077892
  82.8 0.7 copy-start.4
  83.5 0.7 copy-start.5

commit v3 on v2

--- a/solution.py
+++ b/solution.py
@@ -56,13 +56,15 @@
         last = jnp.broadcast_to(p_ref[0, v, :, cells - 1 : cells], (rows, LANES))
         picked = jnp.where(lane == v * rows + line, last, picked)
     face = jnp.sum(picked, axis=0, keepdims=True)
-    face_ref[...] = jnp.broadcast_to(face[None], face_ref.shape)
+    for k in range(face_ref.shape[0]):
+        face_ref[k] = face
     first, final = p_ref[0, :, 0, :], p_ref[0, :, rows - 1, :]
     sibling_ref[...] = jnp.where(upper, first, final)
     outer_ref[...] = jnp.where(upper, final, first)
 
 
-def mix(got_ref, near_ref, mixed_ref, told_ref):
+def mix(got_ref, outer_ref, pair_ref, mixed_ref):
+    del outer_ref, pair_ref
     count, third = got_ref.shape[0], got_ref.shape[1]
     half = count // 2
     deriv = antisymmetric(count)
@@ -80,20 +82,31 @@
             sign = filt if i % 2 == 0 else -filt
             mixed_ref[i, v] = here + sign
             mixed_ref[i + half, v] = (sign if half % 2 == 0 else -sign) - there
-    told_ref[...] = jnp.broadcast_to(near_ref[:, 0, :][None], told_ref.shape)
-
-
-def space(count, p_ref, jac_ref, theta_ref, merid_ref, pair_ref, outer_ref, out_ref, dm_ref):
+
+
+def space(count, p_hbm, jac_hbm, theta_hbm, merid_hbm, pair_ref, outer_ref, out_ref, p_ref, jac_ref, theta_ref, merid_ref, dm_ref, sems):
+    copies = [
+        pltpu.make_async_copy(source, target, sems.at[k])
+        for k, (source, target) in enumerate(
+            [(p_hbm, p_ref), (theta_hbm, theta_ref), (merid_hbm, merid_ref), (jac_hbm, jac_ref)]
+        )
+    ]
+    for copy in copies:
+        copy.start()
     nvar, rows, cells = p_ref.shape[1:]
     core = lax.axis_index(CORE)
     upper = core == 1
     lane = lax.broadcasted_iota(jnp.int32, (rows, cells), 1)
     line = lax.broadcasted_iota(jnp.int32, (rows, LANES), 0)
+    narrow = lax.broadcasted_iota(jnp.int32, (rows, LANES), 1)
+    copies[0].wait()
     for b in range(nvar):
         x = p_ref[0, b]
         right = jnp.where(lane == cells - 1, 0.0, pltpu.roll(x, cells - 1, 1))
         left = jnp.where(lane == 0, 0.0, pltpu.roll(x, 1, 1))
         dm_ref[b] = right - left
+    for copy in copies[1:]:
+        copy.wait()
     for c in range(cells // LANES):
         part = slice(c * LANES, (c + 1) * LANES)
         sibling = pair_ref[1 - core, :, part]
@@ -110,6 +123,8 @@
             dms.append(dm_ref[b, :, part])
         for a in range(nvar):
             acc = (xs[a] - xs[a].astype(jnp.bfloat16).astype(F32)) * (NYQUIST / count)
+            if c == 0:
+                acc = acc + jnp.where(narrow == 0, xs[a], 0.0)
             for b in range(nvar):
                 acc = acc + jac_ref[0, a, b, :, part] * xs[b]
                 acc = acc + theta_ref[a, b] * ths[b]
@@ -117,10 +132,15 @@
             out_ref[a, :, part] = acc
 
 
-def finish(sum_ref, back_ref, faces_ref, p_ref, weights_ref, rows_ref, out_ref, got_ref):
+def finish(sum_ref, back_ref, f0_ref, f1_ref, f2_ref, f3_ref, weights_ref, rows_ref, out_ref, faces_ref, got_ref):
     nvar, rows, cells = sum_ref.shape
     chunks = cells // LANES
     third = nvar // 2
+    near = f0_ref.shape[0]
+    for s, ref in enumerate((f0_ref, f1_ref, f2_ref, f3_ref)):
+        for k in range(near):
+            faces_ref[s * near + k] = ref[k]
+    me = lax.axis_index(FAR)
     for h in range(2):
         for c in range(chunks):
             part = slice(c * LANES, (c + 1) * LANES)
@@ -134,7 +154,8 @@
         for t in range(rows):
             r = rows_ref[0, donor, t]
             device, spot = r // rows, r % rows
-            got_ref[donor, t : t + 1, :] = faces_ref[device // 8, pl.ds(device % 8, 1), :]
+            back = (me + 4 - (device // 2) % 4) % 4
+            got_ref[donor, t : t + 1, :] = faces_ref[back * near + device // 8 * 2 + device % 2]
             within = jnp.where(line == t, spot, within)
         weight = jnp.broadcast_to(weights_ref[0, donor : donor + 1, :], (rows, rows))
         square = (rows, rows)
@@ -145,8 +166,7 @@
         mine = jnp.where(lane // rows == v, total, 0.0)
         interp = jnp.sum(mine, axis=1, keepdims=True)
         head = out_ref[0, v, :, :LANES]
-        interface = p_ref[0, v, :, :LANES] - interp
-        out_ref[0, v, :, :LANES] = head + jnp.where(lane == 0, interface, 0.0)
+        out_ref[0, v, :, :LANES] = head - jnp.where(lane == 0, interp, 0.0)
 
 
 def shards(perturbation, jacobian, flux_theta, flux_merid, donor_rows, donor_weights):
@@ -154,13 +174,14 @@
     ndom = lax.axis_size(DOM)
     _, nvar, rows, cells = perturbation.shape
     smem = pl.BlockSpec(memory_space=pltpu.SMEM)
+    hbm = pl.BlockSpec(memory_space=pltpu.HBM)
     blocks, face, sibling, outer = call(
         prepare,
         (perturbation,),
         whole(1),
         (
             jax.ShapeDtypeStruct((count, nvar // 2, rows, LANES), jnp.bfloat16),
-            jax.ShapeDtypeStruct((far * 2, 8, LANES), F32),
+            jax.ShapeDtypeStruct((ring * 2, 1, LANES), F32),
             jax.ShapeDtypeStruct((nvar, cells), F32),
             jax.ShapeDtypeStruct((nvar, cells), F32),
         ),
@@ -169,39 +190,44 @@
     )
     swaps = [(c, (c + (1 if c % 2 else -1)) % ndom) for c in range(ndom)]
     outer = lax.ppermute(outer, DOM, swaps)
-    near = lax.all_to_all(face, (FAR, CORE), 0, 0, tiled=True)
+    near = lax.all_to_all(face, (RING, CORE), 0, 0, tiled=True)
+    pair = lax.all_gather(sibling, CORE, axis=0)
     got = lax.all_to_all(blocks, INST, 0, 0, tiled=True)
-    pair = lax.all_gather(sibling, CORE, axis=0)
+    mixed = call(
+        mix,
+        (got, outer, pair),
+        whole(1) + [pl.BlockSpec(memory_space=pl.ANY)] * 2,
+        (jax.ShapeDtypeStruct((count, nvar // 2, rows, LANES), F32),),
+        2 * 16 * nvar * rows * cells,
+        "mix",
+    )[0]
+    near, mixed, pair = lax.optimization_barrier((near, mixed, pair))
+    others = [lax.ppermute(near, FAR, [(f, (f + s) % far) for f in range(far)]) for s in range(1, far)]
+    back = lax.all_to_all(mixed, INST, 0, 0, tiled=True)
     total = call(
         functools.partial(space, count),
         (perturbation, jacobian, flux_theta, flux_merid, pair, outer),
-        whole(2) + [smem, smem] + whole(2),
+        [hbm] * 4 + whole(2),
         (jax.ShapeDtypeStruct((nvar, rows, cells), F32),),
         2 * 18 * nvar * rows * cells,
         "space",
-        [pltpu.VMEM((nvar, rows, cells), F32)],
+        [
+            pltpu.VMEM(perturbation.shape, F32),
+            pltpu.VMEM(jacobian.shape, F32),
+            pltpu.SMEM((nvar, nvar), F32),
+            pltpu.SMEM((nvar, nvar), F32),
+            pltpu.VMEM((nvar, rows, cells), F32),
+            pltpu.SemaphoreType.DMA((4,)),
+        ],
     )[0]
-    mixed, told = call(
-        mix,
-        (got, near),
-        whole(2),
-        (
-            jax.ShapeDtypeStruct((count, nvar // 2, rows, LANES), F32),
-            jax.ShapeDtypeStruct((ring, far * 2, LANES), F32),
-        ),
-        2 * 16 * nvar * rows * cells,
-        "mix",
-    )
-    back = lax.all_to_all(mixed, INST, 0, 0, tiled=True)
-    faces = lax.all_to_all(told, RING, 0, 0, tiled=True)
     return call(
         finish,
-        (total, back, faces, perturbation, donor_weights, donor_rows),
-        whole(5) + [smem],
+        (total, back, near) + tuple(others) + (donor_weights, donor_rows),
+        whole(7) + [smem],
         (jax.ShapeDtypeStruct(perturbation.shape, F32),),
         3 * nvar * rows * cells,
         "finish",
-        [pltpu.VMEM((2, rows, LANES), F32)],
+        [pltpu.VMEM((far * ring * 2, 1, LANES), F32), pltpu.VMEM((2, rows, LANES), F32)],
     )[0]
 
 

time: 87.9 us -> 73 us (0.83)
  blocking collectives: 64.2 us -> 1.9 us
  starting transfers between devices: 6.74 us -> 57.2 us
  local copies, waits for them, and re-layouts: 5.04 us -> 2.15 us
  waiting for transfers between devices: 7.14 us -> 5.81 us
  Pallas kernels: 4.25 us -> 5.29 us
    all_to_all x3 -> x0, blocking collectives: 61.9 us -> none  [the longest x1 31.9 us: shards(): near = lax.all_to_all(face, (FAR, CORE), 0, 0, tiled=True)]
    all_to_all x0 -> x2, starting transfers between devices: none -> 20.8 us  [the longest x1 16.5 us: shards(): got = lax.all_to_all(blocks, INST, 0, 0, tiled=True)]
    ppermute x0 -> x3, starting transfers between devices: none -> 17.9 us  [shards(): lax.ppermute(near, FAR, [(f, (f + s) % far) for f in range(far)])]
    ppermute x1, starting transfers between devices: 1.91 us -> 11 us  [shards(): outer = lax.ppermute(outer, DOM, swaps)]
    ppermute x1, waiting for transfers between devices: 7.14 us -> 0.01 us  [shards(): outer = lax.ppermute(outer, DOM, swaps)]
    all_to_all x0 -> x2, waiting for transfers between devices: none -> 4.68 us  [the longest x1 4.67 us: shards(): near = lax.all_to_all(face, (RING, CORE), 0, 0, tiled=True)]
    unnamed x16 -> x14, local copies, waits for them, and re-layouts: 5.04 us -> 2.15 us
    all_to_all x1, starting transfers between devices: 4.83 us -> 7.52 us  [shards(): back = lax.all_to_all(mixed, INST, 0, 0, tiled=True)]
  transfers between devices with their start and end apart: 2 -> 7, of which waited for: 1 -> 2; matrix products, arithmetic and copies ran while one was open for 0% -> 0% of each run, Pallas kernels for 2% -> 4%
where the time goes in v3:
time: 73 us; the launch traced here: 72.5 us
  starting transfers between devices  57.2 us (78%)
  waiting for transfers between devices  5.81 us (8%)
  Pallas kernels  5.29 us (7%)
  local copies, waits for them, and re-layouts  2.15 us (3%)
  blocking collectives  1.9 us (3%)
    ppermute x3, starting transfers between devices, shards(): lax.ppermute(near, FAR, [(f, (f + s) % far) for f in range(far)])  17.9 us
    all_to_all x1, starting transfers between devices, shards(): got = lax.all_to_all(blocks, INST, 0, 0, tiled=True)  16.5 us
    ppermute x1, starting transfers between devices, shards(): outer = lax.ppermute(outer, DOM, swaps)  11 us
    all_to_all x1, starting transfers between devices, shards(): back = lax.all_to_all(mixed, INST, 0, 0, tiled=True)  7.52 us
    pallas_call x4, Pallas kernels, call(): pl.pallas_call(body, out_shape=outs, in_specs=specs, out_specs=whole(len(...  5.29 us
    all_to_all x1, waiting for transfers between devices, shards(): near = lax.all_to_all(face, (RING, CORE), 0, 0, tiled=True)  4.67 us
    all_to_all x1, starting transfers between devices, shards(): near = lax.all_to_all(face, (RING, CORE), 0, 0, tiled=True)  4.31 us
    unnamed x14, local copies, waits for them, and re-layouts  2.15 us
  transfers between devices with their start and end apart: 7, of which 2 were waited for; matrix products, arithmetic and copies ran while one was open for 0% of the time, Pallas kernels for 4%

profile of v3, /device:TPU:2, one launch (start us, length us, event | category | flops | bytes accessed | tf_op | source)
XLA Modules:
  0.0 72.5 jit_solution(8672904766625733320)
XLA Ops:
  0.0 0.0 copy-start
  0.0 0.0 copy-start.1
  0.0 1.1 %copy-done.1 = f32[1,6,16,1024]{3,2,1,0:T(8,128)S(1)} copy-done((f32[1,6,16,1024]{3,2,1,0:T(8,128)S(1)}, f32[1,6,16,1024]{3,2,1,0:T(8,128)}, u32[]{:S(2)}) %copy-start.1) | copy-done | bytes 393240
  1.1 0.0 copy-start.3
  1.2 0.0 copy-start.4
  1.2 0.7 prepare.1
  1.9 16.5 %all-to-all-start.1 = ((bf16[16,3,16,128]{3,2,1,0:T(8,128)(2,1)}), bf16[16,3,16,128]{3,2,1,0:T(8,128)(2,1)S(1)}, u32[]{:S(2)}, u32[]{:S(2)}) async-start(bf16[16,3,16,128]{3,2,1,0:T(8,128)(2,1)} %get-tuple-element.13), calls=%async_computation.1 | async-start | bytes 393216 | tf_op jit(solution)/shard_map/all_to_all | solution.py:195
  18.4 11.0 %collective-permute-start = (f32[6,1024]{1,0:T(8,128)S(1)}, f32[6,1024]{1,0:T(8,128)S(1)}, u32[]{:S(2)}, u32[]{:S(2)}) collective-permute-start(f32[6,1024]{1,0:T(8,128)S(1)} %get-tuple-element.14), channel_id=1, source_target_pairs={{0,63},{1,2},{2,1},{3,4},{4,3},{5,6},{6,5},{7,8},{8,7},{9,10},{10,... | collective-permute-start | bytes 73736 | tf_op jit(solution)/shard_map/ppermute | solution.py:192
  29.4 0.0 all-to-all-done.1.got_ref
  29.4 4.3 %all-to-all-start = ((f32[16,1,128]{2,1,0:T(1,128)}), f32[16,1,128]{2,1,0:T(1,128)S(1)}, u32[]{:S(2)}, u32[]{:S(2)}) async-start(f32[16,1,128]{2,1,0:T(1,128)} %get-tuple-element.12), calls=%async_computation | async-start | bytes 16384 | tf_op jit(solution)/shard_map/all_to_all | solution.py:193
  33.8 1.9 %all-gather.1.pair_ref = f32[2,6,1024]{2,1,0:T(8,128)S(1)} all-gather(f32[1,6,1024]{2,1,0:T(8,128)S(1)} %bitcast.1), channel_id=2, replica_groups=mesh['inst'=16,'ring'=8,'far'=4,'core'=2] {'core'}, dimensions={0}, use_global_device_ids=true | all-gather | bytes 73728 | tf_op jit(solution)/shard_map/all_gather | solution.py:194
  35.7 0.0 copy-start.5
  35.7 0.0 collective-permute-done.outer_ref
  35.7 1.0 %mix.1 = f32[16,3,16,128]{3,2,1,0:T(8,128)} custom-call(bf16[16,3,16,128]{3,2,1,0:T(8,128)(2,1)S(1)} %all-to-all-done.1.got_ref, f32[6,1024]{1,0:T(8,128)S(1)} %collective-permute-done.outer_ref, f32[2,6,1024]{2,1,0:T(8,128)S(1)} %all-gather.1.pair_ref), custom_call_target="tpu_custom_call" | custom-call | flops 3145728 | bytes 663552 | tf_op jit(solution)/shard_map/mix/pallas_call | solution.py:27
  36.7 4.7 %all-to-all-done.f0_ref = f32[16,1,128]{2,1,0:T(1,128)S(1)} async-done(((f32[16,1,128]{2,1,0:T(1,128)}), f32[16,1,128]{2,1,0:T(1,128)S(1)}, u32[]{:S(2)}, u32[]{:S(2)}) %all-to-all-start) | async-done | bytes 8224 | tf_op jit(solution)/shard_map/all_to_all | solution.py:193
  41.3 7.5 %all-to-all-start.2 = ((f32[16,3,16,128]{3,2,1,0:T(8,128)}), f32[16,3,16,128]{3,2,1,0:T(8,128)S(1)}, u32[]{:S(2)}, u32[]{:S(2)}) async-start(f32[16,3,16,128]{3,2,1,0:T(8,128)} %mix.1), calls=%async_computation.2 | async-start | bytes 786432 | tf_op jit(solution)/shard_map/all_to_all | solution.py:206
  48.9 7.3 %collective-permute-start.3 = (f32[16,1,128]{2,1,0:T(1,128)S(1)}, f32[16,1,128]{2,1,0:T(1,128)S(1)}, u32[]{:S(2)}, u32[]{:S(2)}) collective-permute-start(f32[16,1,128]{2,1,0:T(1,128)S(1)} %all-to-all-done.f0_ref), channel_id=1, source_target_pairs={{0,6},{2,0},{4,2},{6,4},{1,7},{3,1},{5,3},{7,5},{8,14},{10,8},{12,... | collective-permute-start | bytes 24584 | tf_op jit(solution)/shard_map/ppermute | solution.py:205
  56.2 4.4 %collective-permute-start.2 = (f32[16,1,128]{2,1,0:T(1,128)S(1)}, f32[16,1,128]{2,1,0:T(1,128)S(1)}, u32[]{:S(2)}, u32[]{:S(2)}) collective-permute-start(f32[16,1,128]{2,1,0:T(1,128)S(1)} %all-to-all-done.f0_ref), channel_id=1, source_target_pairs={{0,4},{2,6},{4,0},{6,2},{1,5},{3,7},{5,1},{7,3},{8,12},{10,14},{12... | collective-permute-start | bytes 24584 | tf_op jit(solution)/shard_map/ppermute | solution.py:205
  60.6 6.1 %collective-permute-start.1 = (f32[16,1,128]{2,1,0:T(1,128)S(1)}, f32[16,1,128]{2,1,0:T(1,128)S(1)}, u32[]{:S(2)}, u32[]{:S(2)}) collective-permute-start(f32[16,1,128]{2,1,0:T(1,128)S(1)} %all-to-all-done.f0_ref), channel_id=1, source_target_pairs={{0,2},{2,4},{4,6},{6,0},{1,3},{3,5},{5,7},{7,1},{8,10},{10,12},{12... | collective-permute-start | bytes 24584 | tf_op jit(solution)/shard_map/ppermute | solution.py:205
  66.7 0.0 copy-done
  66.7 0.0 copy-done.3
  66.8 0.0 copy-done.4
  66.8 0.0 copy-start.2
  66.8 1.0 %copy-done.2 = f32[1,6,16,1024]{3,2,1,0:T(8,128)S(1)} copy-done((f32[1,6,16,1024]{3,2,1,0:T(8,128)S(1)}, f32[1,6,16,1024]{3,2,1,0:T(8,128)}, u32[]{:S(2)}) %copy-start.2) | copy-done | bytes 393240
  67.8 1.6 %space.1.sum_ref = f32[6,16,1024]{2,1,0:T(8,128)S(1)} custom-call(f32[1,6,16,1024]{3,2,1,0:T(8,128)S(1)} %copy-done.2, f32[1,6,6,16,1024]{4,3,2,1,0:T(8,128)S(1)} %copy-done, f32[6,6]{1,0:T(8,128)S(1)} %copy-done.3, f32[6,6]{1,0:T(8,128)S(1)} %copy-done.4, f32[2,6,1024]{2,1,0:T(8,128)S(1)} %all-gather.1.pair_ref, f32[6,1024]{1,0:T(8,128)S(1)} %collective-permute-done.outer_ref), custom_call_target="tpu_custom_call" | custom-call | flops 3538944 | bytes 3219744 | tf_op jit(solution)/shard_map/space/pallas_call | solution.py:27
  69.3 0.0 collective-permute-done.3.f3_ref
  69.3 1.1 %collective-permute-done.2.f2_ref = f32[16,1,128]{2,1,0:T(1,128)S(1)} collective-permute-done((f32[16,1,128]{2,1,0:T(1,128)S(1)}, f32[16,1,128]{2,1,0:T(1,128)S(1)}, u32[]{:S(2)}, u32[]{:S(2)}) %collective-permute-start.2) | collective-permute-done | bytes 8224 | tf_op jit(solution)/shard_map/ppermute | solution.py:205
  70.5 0.0 collective-permute-done.1.f1_ref
  70.5 0.0 all-to-all-done.2.back_ref
  70.5 0.0 copy-done.5
  70.5 0.0 copy-done.6
  70.5 2.0 %finish.1 = f32[1,6,16,1024]{3,2,1,0:T(8,128)} custom-call(f32[6,16,1024]{2,1,0:T(8,128)S(1)} %space.1.sum_ref, f32[16,3,16,128]{3,2,1,0:T(8,128)S(1)} %all-to-all-done.2.back_ref, f32[16,1,128]{2,1,0:T(1,128)S(1)} %all-to-all-done.f0_ref, f32[16,1,128]{2,1,0:T(1,128)S(1)} %collective-permute-done.1.f1_ref, f32[16,1,128]{2,1,0:T(1,128)S(1)} %collective-permute-done.2.f2_ref, ...), custom_call_target="tpu_custom_call" | custom-call | flops 294912 | bytes 1212672 | tf_op jit(solution)/shard_map/finish/pallas_call | solution.py:27
  (1 shorter events, 0.0 us)
Async XLA Ops:
  0.0 66.7 %copy-start = (f32[1,6,6,16,1024]{4,3,2,1,0:T(8,128)S(1)}, f32[1,6,6,16,1024]{4,3,2,1,0:T(8,128)}, u32[]{:S(2)}) copy-start(f32[1,6,6,16,1024]{4,3,2,1,0:T(8,128)} %jac_hbm.1) | copy-start | bytes 7077892
  0.0 1.1 %copy-start.1 = (f32[1,6,16,1024]{3,2,1,0:T(8,128)S(1)}, f32[1,6,16,1024]{3,2,1,0:T(8,128)}, u32[]{:S(2)}) copy-start(f32[1,6,16,1024]{3,2,1,0:T(8,128)} %p_hbm.1) | copy-start | bytes 1179652
  1.1 65.6 %copy-start.3 = (f32[6,6]{1,0:T(8,128)S(1)}, f32[6,6]{1,0:T(8,128)}, u32[]{:S(2)}) copy-start(f32[6,6]{1,0:T(8,128)} %theta_hbm.1) | copy-start | bytes 436
  1.2 65.6 %copy-start.4 = (f32[6,6]{1,0:T(8,128)S(1)}, f32[6,6]{1,0:T(8,128)}, u32[]{:S(2)}) copy-start(f32[6,6]{1,0:T(8,128)} %merid_hbm.1) | copy-start | bytes 436
  1.9 27.6 %all-to-all-start.1 = ((bf16[16,3,16,128]{3,2,1,0:T(8,128)(2,1)}), bf16[16,3,16,128]{3,2,1,0:T(8,128)(2,1)S(1)}, u32[]{:S(2)}, u32[]{:S(2)}) async-start(bf16[16,3,16,128]{3,2,1,0:T(8,128)(2,1)} %get-tuple-element.13), calls=%async_computation.1 | async-start | bytes 393216 | tf_op jit(solution)/shard_map/all_to_all | solution.py:195
  18.4 17.3 %collective-permute-start = (f32[6,1024]{1,0:T(8,128)S(1)}, f32[6,1024]{1,0:T(8,128)S(1)}, u32[]{:S(2)}, u32[]{:S(2)}) collective-permute-start(f32[6,1024]{1,0:T(8,128)S(1)} %get-tuple-element.14), channel_id=1, source_target_pairs={{0,63},{1,2},{2,1},{3,4},{4,3},{5,6},{6,5},{7,8},{8,7},{9,10},{10,... | collective-permute-start | bytes 73736 | tf_op jit(solution)/shard_map/ppermute | solution.py:192
  29.4 11.9 %all-to-all-start = ((f32[16,1,128]{2,1,0:T(1,128)}), f32[16,1,128]{2,1,0:T(1,128)S(1)}, u32[]{:S(2)}, u32[]{:S(2)}) async-start(f32[16,1,128]{2,1,0:T(1,128)} %get-tuple-element.12), calls=%async_computation | async-start | bytes 16384 | tf_op jit(solution)/shard_map/all_to_all | solution.py:193
  35.7 34.8 %copy-start.5 = (f32[1,2,16]{2,1,0:T(2,128)S(1)}, f32[1,2,16]{2,1,0:T(2,128)}, u32[]{:S(2)}) copy-start(f32[1,2,16]{2,1,0:T(2,128)} %weights_ref.1) | copy-start | bytes 388
  35.7 34.8 %copy-start.6 = (s32[1,2,16]{2,1,0:T(2,128)S(1)}, s32[1,2,16]{2,1,0:T(2,128)}, u32[]{:S(2)}) copy-start(s32[1,2,16]{2,1,0:T(2,128)} %rows_ref.1) | copy-start | bytes 388
  41.3 29.1 %all-to-all-start.2 = ((f32[16,3,16,128]{3,2,1,0:T(8,128)}), f32[16,3,16,128]{3,2,1,0:T(8,128)S(1)}, u32[]{:S(2)}, u32[]{:S(2)}) async-start(f32[16,3,16,128]{3,2,1,0:T(8,128)} %mix.1), calls=%async_computation.2 | async-start | bytes 786432 | tf_op jit(solution)/shard_map/all_to_all | solution.py:206
  48.9 20.5 %collective-permute-start.3 = (f32[16,1,128]{2,1,0:T(1,128)S(1)}, f32[16,1,128]{2,1,0:T(1,128)S(1)}, u32[]{:S(2)}, u32[]{:S(2)}) collective-permute-start(f32[16,1,128]{2,1,0:T(1,128)S(1)} %all-to-all-done.f0_ref), channel_id=1, source_target_pairs={{0,6},{2,0},{4,2},{6,4},{1,7},{3,1},{5,3},{7,5},{8,14},{10,8},{12,... | collective-permute-start | bytes 24584 | tf_op jit(solution)/shard_map/ppermute | solution.py:205
  56.2 14.3 %collective-permute-start.2 = (f32[16,1,128]{2,1,0:T(1,128)S(1)}, f32[16,1,128]{2,1,0:T(1,128)S(1)}, u32[]{:S(2)}, u32[]{:S(2)}) collective-permute-start(f32[16,1,128]{2,1,0:T(1,128)S(1)} %all-to-all-done.f0_ref), channel_id=1, source_target_pairs={{0,4},{2,6},{4,0},{6,2},{1,5},{3,7},{5,1},{7,3},{8,12},{10,14},{12... | collective-permute-start | bytes 24584 | tf_op jit(solution)/shard_map/ppermute | solution.py:205
  60.6 9.8 %collective-permute-start.1 = (f32[16,1,128]{2,1,0:T(1,128)S(1)}, f32[16,1,128]{2,1,0:T(1,128)S(1)}, u32[]{:S(2)}, u32[]{:S(2)}) collective-permute-start(f32[16,1,128]{2,1,0:T(1,128)S(1)} %all-to-all-done.f0_ref), channel_id=1, source_target_pairs={{0,2},{2,4},{4,6},{6,0},{1,3},{3,5},{5,7},{7,1},{8,10},{10,12},{12... | collective-permute-start | bytes 24584 | tf_op jit(solution)/shard_map/ppermute | solution.py:205
  66.8 1.0 %copy-start.2 = (f32[1,6,16,1024]{3,2,1,0:T(8,128)S(1)}, f32[1,6,16,1024]{3,2,1,0:T(8,128)}, u32[]{:S(2)}) copy-start(f32[1,6,16,1024]{3,2,1,0:T(8,128)} %p_hbm.1) | copy-start | bytes 1179652

commit v4 on v3

--- a/solution.py
+++ b/solution.py
@@ -22,13 +22,13 @@
     return [pl.BlockSpec(memory_space=pltpu.VMEM) for _ in range(count)]
 
 
-def call(body, operands, specs, outs, flops, name, scratch=()):
+def call(body, operands, specs, outs, flops, name, scratch=(), out_specs=None):
     moved = sum(math.prod(v.shape) * v.dtype.itemsize for v in list(operands) + list(outs))
     return pl.pallas_call(
         body,
         out_shape=outs,
         in_specs=specs,
-        out_specs=whole(len(outs)),
+        out_specs=out_specs or whole(len(outs)),
         scratch_shapes=scratch,
         compiler_params=pltpu.CompilerParams(vmem_limit_bytes=VMEM_BYTES),
         cost_estimate=pl.CostEstimate(flops=flops, bytes_accessed=moved, transcendentals=0),
@@ -84,7 +84,7 @@
             mixed_ref[i + half, v] = (sign if half % 2 == 0 else -sign) - there
 
 
-def space(count, p_hbm, jac_hbm, theta_hbm, merid_hbm, pair_ref, outer_ref, out_ref, p_ref, jac_ref, theta_ref, merid_ref, dm_ref, sems):
+def space(count, p_hbm, jac_hbm, theta_hbm, merid_hbm, pair_ref, outer_ref, rows_ref, weights_ref, out_ref, select_ref, within_ref, p_ref, jac_ref, theta_ref, merid_ref, dm_ref, sems):
     copies = [
         pltpu.make_async_copy(source, target, sems.at[k])
         for k, (source, target) in enumerate(
@@ -99,6 +99,19 @@
     lane = lax.broadcasted_iota(jnp.int32, (rows, cells), 1)
     line = lax.broadcasted_iota(jnp.int32, (rows, LANES), 0)
     narrow = lax.broadcasted_iota(jnp.int32, (rows, LANES), 1)
+    square = (rows, rows)
+    eye = lax.broadcasted_iota(jnp.int32, square, 0) == lax.broadcasted_iota(jnp.int32, square, 1)
+    places = lax.broadcasted_iota(jnp.int32, select_ref.shape[1:], 1)
+    me = lax.axis_index(FAR)
+    for donor in range(2):
+        given = jnp.broadcast_to(rows_ref[0, donor : donor + 1, :], square)
+        given = jnp.sum(jnp.where(eye, given, 0).astype(F32), axis=1, keepdims=True).astype(jnp.int32)
+        weight = jnp.broadcast_to(weights_ref[0, donor : donor + 1, :], square)
+        weight = jnp.sum(jnp.where(eye, weight, 0.0), axis=1, keepdims=True)
+        device, spot = given >> 4, given & 15
+        place = (((device >> 1) & 3) ^ me) * 16 + (device >> 3) * 2 + (device & 1)
+        select_ref[donor] = jnp.where(places == place, weight, 0.0)
+        within_ref[donor] = jnp.where((narrow & 15) == spot, 1.0, 0.0)
     copies[0].wait()
     for b in range(nvar):
         x = p_ref[0, b]
@@ -132,48 +145,39 @@
             out_ref[a, :, part] = acc
 
 
-def finish(sum_ref, back_ref, f0_ref, f1_ref, f2_ref, f3_ref, weights_ref, rows_ref, out_ref, faces_ref, got_ref):
+def finish(sum_ref, back_ref, f0_ref, f1_ref, f2_ref, f3_ref, select_ref, within_ref, out_hbm, out_ref, faces_ref, sems):
     nvar, rows, cells = sum_ref.shape
     chunks = cells // LANES
     third = nvar // 2
     near = f0_ref.shape[0]
     for s, ref in enumerate((f0_ref, f1_ref, f2_ref, f3_ref)):
         for k in range(near):
-            faces_ref[s * near + k] = ref[k]
-    me = lax.axis_index(FAR)
-    for h in range(2):
-        for c in range(chunks):
-            part = slice(c * LANES, (c + 1) * LANES)
-            own = slice(h * third, (h + 1) * third)
-            out_ref[0, own, :, part] = sum_ref[own, :, part] + back_ref[h * chunks + c]
+            faces_ref[s * near + k : s * near + k + 1, :] = ref[k]
     lane = lax.broadcasted_iota(jnp.int32, (rows, LANES), 1)
-    line = lax.broadcasted_iota(jnp.int32, (rows, LANES), 0)
     total = jnp.zeros((rows, LANES), F32)
     for donor in range(2):
-        within = jnp.zeros((rows, LANES), jnp.int32)
-        for t in range(rows):
-            r = rows_ref[0, donor, t]
-            device, spot = r // rows, r % rows
-            back = (me + 4 - (device // 2) % 4) % 4
-            got_ref[donor, t : t + 1, :] = faces_ref[back * near + device // 8 * 2 + device % 2]
-            within = jnp.where(line == t, spot, within)
-        weight = jnp.broadcast_to(weights_ref[0, donor : donor + 1, :], (rows, rows))
-        square = (rows, rows)
-        eye = lax.broadcasted_iota(jnp.int32, square, 0) == lax.broadcasted_iota(jnp.int32, square, 1)
-        weight = jnp.sum(jnp.where(eye, weight, 0.0), axis=1, keepdims=True)
-        total = total + jnp.where(lane % rows == within, got_ref[donor], 0.0) * weight
+        picked = jnp.dot(
+            select_ref[donor], faces_ref[...], precision=lax.Precision.HIGHEST, preferred_element_type=F32
+        )
+        total = total + picked * within_ref[donor]
+    copies = []
     for v in range(nvar):
         mine = jnp.where(lane // rows == v, total, 0.0)
         interp = jnp.sum(mine, axis=1, keepdims=True)
-        head = out_ref[0, v, :, :LANES]
-        out_ref[0, v, :, :LANES] = head - jnp.where(lane == 0, interp, 0.0)
+        for c in range(chunks):
+            part = slice(c * LANES, (c + 1) * LANES)
+            both = sum_ref[v, :, part] + back_ref[v // third * chunks + c, v % third]
+            out_ref[v, :, part] = both - jnp.where(lane == 0, interp, 0.0) if c == 0 else both
+        copies.append(pltpu.make_async_copy(out_ref.at[v], out_hbm.at[0, v], sems.at[v]))
+        copies[v].start()
+    for copy in copies:
+        copy.wait()
 
 
 def shards(perturbation, jacobian, flux_theta, flux_merid, donor_rows, donor_weights):
     count, far, ring = lax.axis_size(INST), lax.axis_size(FAR), lax.axis_size(RING)
     ndom = lax.axis_size(DOM)
     _, nvar, rows, cells = perturbation.shape
-    smem = pl.BlockSpec(memory_space=pltpu.SMEM)
     hbm = pl.BlockSpec(memory_space=pltpu.HBM)
     blocks, face, sibling, outer = call(
         prepare,
@@ -202,13 +206,17 @@
         "mix",
     )[0]
     near, mixed, pair = lax.optimization_barrier((near, mixed, pair))
-    others = [lax.ppermute(near, FAR, [(f, (f + s) % far) for f in range(far)]) for s in range(1, far)]
+    others = [lax.ppermute(near, FAR, [(f, f ^ s) for f in range(far)]) for s in range(1, far)]
     back = lax.all_to_all(mixed, INST, 0, 0, tiled=True)
-    total = call(
+    total, select, within = call(
         functools.partial(space, count),
-        (perturbation, jacobian, flux_theta, flux_merid, pair, outer),
-        [hbm] * 4 + whole(2),
-        (jax.ShapeDtypeStruct((nvar, rows, cells), F32),),
+        (perturbation, jacobian, flux_theta, flux_merid, pair, outer, donor_rows, donor_weights),
+        [hbm] * 4 + whole(4),
+        (
+            jax.ShapeDtypeStruct((nvar, rows, cells), F32),
+            jax.ShapeDtypeStruct((2, rows, far * ring * 2), F32),
+            jax.ShapeDtypeStruct((2, rows, LANES), F32),
+        ),
         2 * 18 * nvar * rows * cells,
         "space",
         [
@@ -219,15 +227,20 @@
             pltpu.VMEM((nvar, rows, cells), F32),
             pltpu.SemaphoreType.DMA((4,)),
         ],
-    )[0]
+    )
     return call(
         finish,
-        (total, back, near) + tuple(others) + (donor_weights, donor_rows),
-        whole(7) + [smem],
+        (total, back, near) + tuple(others) + (select, within),
+        whole(8),
         (jax.ShapeDtypeStruct(perturbation.shape, F32),),
         3 * nvar * rows * cells,
         "finish",
-        [pltpu.VMEM((far * ring * 2, 1, LANES), F32), pltpu.VMEM((2, rows, LANES), F32)],
+        [
+            pltpu.VMEM((nvar, rows, cells), F32),
+            pltpu.VMEM((far * ring * 2, LANES), F32),
+            pltpu.SemaphoreType.DMA((nvar,)),
+        ],
+        [hbm],
     )[0]
 
 

time: 73 us -> 72.1 us (0.988)
  Pallas kernels: 5.29 us -> 4.32 us
  waiting for transfers between devices: 5.81 us -> 6.65 us
    pallas_call x4, Pallas kernels: 5.29 us -> 4.32 us  [call(): pl.pallas_call(body, out_shape=outs, in_specs=specs, out_specs=out_specs...]
    ppermute x3, waiting for transfers between devices: 1.13 us -> 1.99 us  [shards(): lax.ppermute(near, FAR, [(f, f ^ s) for f in range(far)])]
    ppermute x3, starting transfers between devices: 17.9 us -> 17 us  [shards(): lax.ppermute(near, FAR, [(f, f ^ s) for f in range(far)])]
where the time goes in v4:
time: 72.1 us; the launch traced here: 71.5 us
  starting transfers between devices  56.5 us (78%)
  waiting for transfers between devices  6.65 us (9%)
  Pallas kernels  4.32 us (6%)
  local copies, waits for them, and re-layouts  2.01 us (3%)
  blocking collectives  1.9 us (3%)
    ppermute x3, starting transfers between devices, shards(): lax.ppermute(near, FAR, [(f, f ^ s) for f in range(far)])  17 us
    all_to_all x1, starting transfers between devices, shards(): got = lax.all_to_all(blocks, INST, 0, 0, tiled=True)  16.6 us
    ppermute x1, starting transfers between devices, shards(): outer = lax.ppermute(outer, DOM, swaps)  11 us
    all_to_all x1, starting transfers between devices, shards(): back = lax.all_to_all(mixed, INST, 0, 0, tiled=True)  7.52 us
    all_to_all x1, waiting for transfers between devices, shards(): near = lax.all_to_all(face, (RING, CORE), 0, 0, tiled=True)  4.66 us
    pallas_call x4, Pallas kernels, call(): pl.pallas_call(body, out_shape=outs, in_specs=specs, out_specs=out_specs...  4.32 us
    all_to_all x1, starting transfers between devices, shards(): near = lax.all_to_all(face, (RING, CORE), 0, 0, tiled=True)  4.31 us
    unnamed x14, local copies, waits for them, and re-layouts  2.01 us
  transfers between devices with their start and end apart: 7, of which 2 were waited for; matrix products, arithmetic and copies ran while one was open for 0% of the time, Pallas kernels for 4%

profile of v4, /device:TPU:2, one launch (start us, length us, event | category | flops | bytes accessed | tf_op | source)
XLA Modules:
  0.0 71.5 jit_solution(1815881923631990844)
XLA Ops:
  0.0 0.0 copy-start.1
  0.0 1.0 %copy-done.1 = f32[1,6,16,1024]{3,2,1,0:T(8,128)S(1)} copy-done((f32[1,6,16,1024]{3,2,1,0:T(8,128)S(1)}, f32[1,6,16,1024]{3,2,1,0:T(8,128)}, u32[]{:S(2)}) %copy-start.1) | copy-done | bytes 393240
  1.0 0.0 copy-start
  1.0 0.0 copy-start.3
  1.0 0.0 copy-start.4
  1.0 0.0 copy-start.6
  1.0 0.7 %prepare.1 = (bf16[16,3,16,128]{3,2,1,0:T(8,128)(2,1)}, f32[16,1,128]{2,1,0:T(1,128)}, f32[6,1024]{1,0:T(8,128)S(1)}, f32[6,1024]{1,0:T(8,128)S(1)}) custom-call(f32[1,6,16,1024]{3,2,1,0:T(8,128)S(1)} %copy-done.1), custom_call_target="tpu_custom_call" | custom-call | flops 1000000 | bytes 647168 | tf_op jit(solution)/shard_map/prepare/pallas_call | solution.py:27
  1.7 16.6 %all-to-all-start.1 = ((bf16[16,3,16,128]{3,2,1,0:T(8,128)(2,1)}), bf16[16,3,16,128]{3,2,1,0:T(8,128)(2,1)S(1)}, u32[]{:S(2)}, u32[]{:S(2)}) async-start(bf16[16,3,16,128]{3,2,1,0:T(8,128)(2,1)} %get-tuple-element.16), calls=%async_computation.1 | async-start | bytes 393216 | tf_op jit(solution)/shard_map/all_to_all | solution.py:199
  18.4 11.0 %collective-permute-start = (f32[6,1024]{1,0:T(8,128)S(1)}, f32[6,1024]{1,0:T(8,128)S(1)}, u32[]{:S(2)}, u32[]{:S(2)}) collective-permute-start(f32[6,1024]{1,0:T(8,128)S(1)} %get-tuple-element.17), channel_id=1, source_target_pairs={{0,63},{1,2},{2,1},{3,4},{4,3},{5,6},{6,5},{7,8},{8,7},{9,10},{10,... | collective-permute-start | bytes 73736 | tf_op jit(solution)/shard_map/ppermute | solution.py:196
  29.4 0.0 all-to-all-done.1.got_ref
  29.4 4.3 %all-to-all-start = ((f32[16,1,128]{2,1,0:T(1,128)}), f32[16,1,128]{2,1,0:T(1,128)S(1)}, u32[]{:S(2)}, u32[]{:S(2)}) async-start(f32[16,1,128]{2,1,0:T(1,128)} %get-tuple-element.15), calls=%async_computation | async-start | bytes 16384 | tf_op jit(solution)/shard_map/all_to_all | solution.py:197
  33.8 1.9 %all-gather.1.pair_ref = f32[2,6,1024]{2,1,0:T(8,128)S(1)} all-gather(f32[1,6,1024]{2,1,0:T(8,128)S(1)} %bitcast.1), channel_id=2, replica_groups=mesh['inst'=16,'ring'=8,'far'=4,'core'=2] {'core'}, dimensions={0}, use_global_device_ids=true | all-gather | bytes 73728 | tf_op jit(solution)/shard_map/all_gather | solution.py:198
  35.7 0.0 collective-permute-done.outer_ref
  35.7 1.0 %mix.1 = f32[16,3,16,128]{3,2,1,0:T(8,128)} custom-call(bf16[16,3,16,128]{3,2,1,0:T(8,128)(2,1)S(1)} %all-to-all-done.1.got_ref, f32[6,1024]{1,0:T(8,128)S(1)} %collective-permute-done.outer_ref, f32[2,6,1024]{2,1,0:T(8,128)S(1)} %all-gather.1.pair_ref), custom_call_target="tpu_custom_call" | custom-call | flops 3145728 | bytes 663552 | tf_op jit(solution)/shard_map/mix/pallas_call | solution.py:27
  36.7 4.7 %all-to-all-done.f0_ref = f32[16,1,128]{2,1,0:T(1,128)S(1)} async-done(((f32[16,1,128]{2,1,0:T(1,128)}), f32[16,1,128]{2,1,0:T(1,128)S(1)}, u32[]{:S(2)}, u32[]{:S(2)}) %all-to-all-start) | async-done | bytes 8224 | tf_op jit(solution)/shard_map/all_to_all | solution.py:197
  41.3 7.5 %all-to-all-start.2 = ((f32[16,3,16,128]{3,2,1,0:T(8,128)}), f32[16,3,16,128]{3,2,1,0:T(8,128)S(1)}, u32[]{:S(2)}, u32[]{:S(2)}) async-start(f32[16,3,16,128]{3,2,1,0:T(8,128)} %mix.1), calls=%async_computation.2 | async-start | bytes 786432 | tf_op jit(solution)/shard_map/all_to_all | solution.py:210
  48.8 7.3 %collective-permute-start.3 = (f32[16,1,128]{2,1,0:T(1,128)S(1)}, f32[16,1,128]{2,1,0:T(1,128)S(1)}, u32[]{:S(2)}, u32[]{:S(2)}) collective-permute-start(f32[16,1,128]{2,1,0:T(1,128)S(1)} %all-to-all-done.f0_ref), channel_id=1, source_target_pairs={{0,6},{2,4},{4,2},{6,0},{1,7},{3,5},{5,3},{7,1},{8,14},{10,12},{12... | collective-permute-start | bytes 24584 | tf_op jit(solution)/shard_map/ppermute | solution.py:209
  56.2 4.4 %collective-permute-start.2 = (f32[16,1,128]{2,1,0:T(1,128)S(1)}, f32[16,1,128]{2,1,0:T(1,128)S(1)}, u32[]{:S(2)}, u32[]{:S(2)}) collective-permute-start(f32[16,1,128]{2,1,0:T(1,128)S(1)} %all-to-all-done.f0_ref), channel_id=1, source_target_pairs={{0,4},{2,6},{4,0},{6,2},{1,5},{3,7},{5,1},{7,3},{8,12},{10,14},{12... | collective-permute-start | bytes 24584 | tf_op jit(solution)/shard_map/ppermute | solution.py:209
  60.6 5.3 %collective-permute-start.1 = (f32[16,1,128]{2,1,0:T(1,128)S(1)}, f32[16,1,128]{2,1,0:T(1,128)S(1)}, u32[]{:S(2)}, u32[]{:S(2)}) collective-permute-start(f32[16,1,128]{2,1,0:T(1,128)S(1)} %all-to-all-done.f0_ref), channel_id=1, source_target_pairs={{0,2},{2,0},{4,6},{6,4},{1,3},{3,1},{5,7},{7,5},{8,10},{10,8},{12,... | collective-permute-start | bytes 24584 | tf_op jit(solution)/shard_map/ppermute | solution.py:209
  65.9 0.0 copy-done
  65.9 0.0 copy-done.3
  65.9 0.0 copy-done.4
  65.9 0.0 copy-done.5
  65.9 0.0 copy-done.6
  65.9 0.0 copy-start.2
  65.9 1.0 %copy-done.2 = f32[1,6,16,1024]{3,2,1,0:T(8,128)S(1)} copy-done((f32[1,6,16,1024]{3,2,1,0:T(8,128)S(1)}, f32[1,6,16,1024]{3,2,1,0:T(8,128)}, u32[]{:S(2)}) %copy-start.2) | copy-done | bytes 393240
  66.9 1.6 %space.1 = (f32[6,16,1024]{2,1,0:T(8,128)S(1)}, f32[2,16,64]{2,1,0:T(8,128)S(1)}, f32[2,16,128]{2,1,0:T(8,128)S(1)}) custom-call(f32[1,6,16,1024]{3,2,1,0:T(8,128)S(1)} %copy-done.2, f32[1,6,6,16,1024]{4,3,2,1,0:T(8,128)S(1)} %copy-done, f32[6,6]{1,0:T(8,128)S(1)} %copy-done.3, f32[6,6]{1,0:T(8,128)S(1)} %copy-done.4, f32[2,6,1024]{2,1,0:T(8,128)S(1)} %all-gather.1.pair_ref, ...), custom_call_target="tpu_custom_call" | custom-call | flops 3538944 | bytes 3244576 | tf_op jit(solution)/shard_map/space/pallas_call | solution.py:27
  68.5 0.0 collective-permute-done.3.f3_ref
  68.5 2.0 %collective-permute-done.2.f2_ref = f32[16,1,128]{2,1,0:T(1,128)S(1)} collective-permute-done((f32[16,1,128]{2,1,0:T(1,128)S(1)}, f32[16,1,128]{2,1,0:T(1,128)S(1)}, u32[]{:S(2)}, u32[]{:S(2)}) %collective-permute-start.2) | collective-permute-done | bytes 8224 | tf_op jit(solution)/shard_map/ppermute | solution.py:209
  70.5 0.0 collective-permute-done.1.f1_ref
  70.5 0.0 all-to-all-done.2.back_ref
  70.5 1.0 %finish.1 = f32[1,6,16,1024]{3,2,1,0:T(8,128)} custom-call(f32[6,16,1024]{2,1,0:T(8,128)S(1)} %get-tuple-element.20.sum_ref, f32[16,3,16,128]{3,2,1,0:T(8,128)S(1)} %all-to-all-done.2.back_ref, f32[16,1,128]{2,1,0:T(1,128)S(1)} %all-to-all-done.f0_ref, f32[16,1,128]{2,1,0:T(1,128)S(1)} %collective-permute-done.1.f1_ref, ...), custom_call_target="tpu_custom_call" | custom-call | flops 294912 | bytes 1236992 | tf_op jit(solution)/shard_map/finish/pallas_call | solution.py:27
  (1 shorter events, 0.0 us)
Async XLA Ops:
  0.0 1.0 %copy-start.1 = (f32[1,6,16,1024]{3,2,1,0:T(8,128)S(1)}, f32[1,6,16,1024]{3,2,1,0:T(8,128)}, u32[]{:S(2)}) copy-start(f32[1,6,16,1024]{3,2,1,0:T(8,128)} %p_hbm.1) | copy-start | bytes 1179652
  1.0 64.9 %copy-start = (f32[1,6,6,16,1024]{4,3,2,1,0:T(8,128)S(1)}, f32[1,6,6,16,1024]{4,3,2,1,0:T(8,128)}, u32[]{:S(2)}) copy-start(f32[1,6,6,16,1024]{4,3,2,1,0:T(8,128)} %jac_hbm.1) | copy-start | bytes 7077892
  1.0 64.9 %copy-start.3 = (f32[6,6]{1,0:T(8,128)S(1)}, f32[6,6]{1,0:T(8,128)}, u32[]{:S(2)}) copy-start(f32[6,6]{1,0:T(8,128)} %theta_hbm.1) | copy-start | bytes 436
  1.0 64.9 %copy-start.4 = (f32[6,6]{1,0:T(8,128)S(1)}, f32[6,6]{1,0:T(8,128)}, u32[]{:S(2)}) copy-start(f32[6,6]{1,0:T(8,128)} %merid_hbm.1) | copy-start | bytes 436
  1.0 64.9 %copy-start.5 = (s32[1,2,16]{2,1,0:T(2,128)S(1)}, s32[1,2,16]{2,1,0:T(2,128)}, u32[]{:S(2)}) copy-start(s32[1,2,16]{2,1,0:T(2,128)} %rows_ref.1) | copy-start | bytes 388
  1.0 64.9 %copy-start.6 = (f32[1,2,16]{2,1,0:T(2,128)S(1)}, f32[1,2,16]{2,1,0:T(2,128)}, u32[]{:S(2)}) copy-start(f32[1,2,16]{2,1,0:T(2,128)} %weights_ref.1) | copy-start | bytes 388
  1.7 27.7 %all-to-all-start.1 = ((bf16[16,3,16,128]{3,2,1,0:T(8,128)(2,1)}), bf16[16,3,16,128]{3,2,1,0:T(8,128)(2,1)S(1)}, u32[]{:S(2)}, u32[]{:S(2)}) async-start(bf16[16,3,16,128]{3,2,1,0:T(8,128)(2,1)} %get-tuple-element.16), calls=%async_computation.1 | async-start | bytes 393216 | tf_op jit(solution)/shard_map/all_to_all | solution.py:199
  18.4 17.3 %collective-permute-start = (f32[6,1024]{1,0:T(8,128)S(1)}, f32[6,1024]{1,0:T(8,128)S(1)}, u32[]{:S(2)}, u32[]{:S(2)}) collective-permute-start(f32[6,1024]{1,0:T(8,128)S(1)} %get-tuple-element.17), channel_id=1, source_target_pairs={{0,63},{1,2},{2,1},{3,4},{4,3},{5,6},{6,5},{7,8},{8,7},{9,10},{10,... | collective-permute-start | bytes 73736 | tf_op jit(solution)/shard_map/ppermute | solution.py:196
  29.4 11.9 %all-to-all-start = ((f32[16,1,128]{2,1,0:T(1,128)}), f32[16,1,128]{2,1,0:T(1,128)S(1)}, u32[]{:S(2)}, u32[]{:S(2)}) async-start(f32[16,1,128]{2,1,0:T(1,128)} %get-tuple-element.15), calls=%async_computation | async-start | bytes 16384 | tf_op jit(solution)/shard_map/all_to_all | solution.py:197
  41.3 29.2 %all-to-all-start.2 = ((f32[16,3,16,128]{3,2,1,0:T(8,128)}), f32[16,3,16,128]{3,2,1,0:T(8,128)S(1)}, u32[]{:S(2)}, u32[]{:S(2)}) async-start(f32[16,3,16,128]{3,2,1,0:T(8,128)} %mix.1), calls=%async_computation.2 | async-start | bytes 786432 | tf_op jit(solution)/shard_map/all_to_all | solution.py:210
  48.8 19.7 %collective-permute-start.3 = (f32[16,1,128]{2,1,0:T(1,128)S(1)}, f32[16,1,128]{2,1,0:T(1,128)S(1)}, u32[]{:S(2)}, u32[]{:S(2)}) collective-permute-start(f32[16,1,128]{2,1,0:T(1,128)S(1)} %all-to-all-done.f0_ref), channel_id=1, source_target_pairs={{0,6},{2,4},{4,2},{6,0},{1,7},{3,5},{5,3},{7,1},{8,14},{10,12},{12... | collective-permute-start | bytes 24584 | tf_op jit(solution)/shard_map/ppermute | solution.py:209
  56.2 14.3 %collective-permute-start.2 = (f32[16,1,128]{2,1,0:T(1,128)S(1)}, f32[16,1,128]{2,1,0:T(1,128)S(1)}, u32[]{:S(2)}, u32[]{:S(2)}) collective-permute-start(f32[16,1,128]{2,1,0:T(1,128)S(1)} %all-to-all-done.f0_ref), channel_id=1, source_target_pairs={{0,4},{2,6},{4,0},{6,2},{1,5},{3,7},{5,1},{7,3},{8,12},{10,14},{12... | collective-permute-start | bytes 24584 | tf_op jit(solution)/shard_map/ppermute | solution.py:209
  60.6 9.9 %collective-permute-start.1 = (f32[16,1,128]{2,1,0:T(1,128)S(1)}, f32[16,1,128]{2,1,0:T(1,128)S(1)}, u32[]{:S(2)}, u32[]{:S(2)}) collective-permute-start(f32[16,1,128]{2,1,0:T(1,128)S(1)} %all-to-all-done.f0_ref), channel_id=1, source_target_pairs={{0,2},{2,0},{4,6},{6,4},{1,3},{3,1},{5,7},{7,5},{8,10},{10,8},{12,... | collective-permute-start | bytes 24584 | tf_op jit(solution)/shard_map/ppermute | solution.py:209
  65.9 1.0 %copy-start.2 = (f32[1,6,16,1024]{3,2,1,0:T(8,128)S(1)}, f32[1,6,16,1024]{3,2,1,0:T(8,128)}, u32[]{:S(2)}) copy-start(f32[1,6,16,1024]{3,2,1,0:T(8,128)} %p_hbm.1) | copy-start | bytes 1179652

commit v5 on v4

--- a/solution.py
+++ b/solution.py
@@ -22,10 +22,11 @@
     return [pl.BlockSpec(memory_space=pltpu.VMEM) for _ in range(count)]
 
 
-def call(body, operands, specs, outs, flops, name, scratch=(), out_specs=None):
+def call(body, operands, specs, outs, flops, name, scratch=(), out_specs=None, grid=()):
     moved = sum(math.prod(v.shape) * v.dtype.itemsize for v in list(operands) + list(outs))
     return pl.pallas_call(
         body,
+        grid=grid,
         out_shape=outs,
         in_specs=specs,
         out_specs=out_specs or whole(len(outs)),
@@ -41,26 +42,28 @@
 
 
 def prepare(p_ref, blocks_ref, face_ref, sibling_ref, outer_ref):
-    nvar, rows, cells = p_ref.shape[1:]
-    chunks = cells // LANES
+    third, rows, cells = p_ref.shape[1:]
     upper = lax.axis_index(CORE) == 1
     low = p_ref[0].astype(jnp.bfloat16)
-    third = nvar // 2
-    for h in range(2):
-        for c in range(chunks):
-            blocks_ref[h * chunks + c] = low[h * third : (h + 1) * third, :, c * LANES : (c + 1) * LANES]
+    for c in range(cells // LANES):
+        blocks_ref[c] = low[:, :, c * LANES : (c + 1) * LANES]
     lane = lax.broadcasted_iota(jnp.int32, (rows, LANES), 1)
     line = lax.broadcasted_iota(jnp.int32, (rows, LANES), 0)
-    picked = jnp.zeros((rows, LANES), F32)
-    for v in range(nvar):
-        last = jnp.broadcast_to(p_ref[0, v, :, cells - 1 : cells], (rows, LANES))
-        picked = jnp.where(lane == v * rows + line, last, picked)
-    face = jnp.sum(picked, axis=0, keepdims=True)
-    for k in range(face_ref.shape[0]):
-        face_ref[k] = face
-    first, final = p_ref[0, :, 0, :], p_ref[0, :, rows - 1, :]
-    sibling_ref[...] = jnp.where(upper, first, final)
-    outer_ref[...] = jnp.where(upper, final, first)
+
+    def rest(h):
+        picked = jnp.zeros((rows, LANES), F32)
+        for v in range(third):
+            last = jnp.broadcast_to(p_ref[0, v, :, cells - 1 : cells], (rows, LANES))
+            picked = jnp.where(lane == (h * third + v) * rows + line, last, picked)
+        face = jnp.sum(picked, axis=0, keepdims=True)
+        for k in range(face_ref.shape[0]):
+            face_ref[k] = face if h == 0 else face_ref[k] + face
+        first, final = p_ref[0, :, 0, :], p_ref[0, :, rows - 1, :]
+        sibling_ref[h * third : (h + 1) * third] = jnp.where(upper, first, final)
+        outer_ref[h * third : (h + 1) * third] = jnp.where(upper, final, first)
+
+    pl.when(pl.program_id(0) == 0)(lambda: rest(0))
+    pl.when(pl.program_id(0) == 1)(lambda: rest(1))
 
 
 def mix(got_ref, outer_ref, pair_ref, mixed_ref):
@@ -145,7 +148,7 @@
             out_ref[a, :, part] = acc
 
 
-def finish(sum_ref, back_ref, f0_ref, f1_ref, f2_ref, f3_ref, select_ref, within_ref, out_hbm, out_ref, faces_ref, sems):
+def finish(sum_ref, back_ref, f0_ref, f1_ref, f3_ref, f2_ref, select_ref, within_ref, out_hbm, out_ref, faces_ref, sems):
     nvar, rows, cells = sum_ref.shape
     chunks = cells // LANES
     third = nvar // 2
@@ -182,7 +185,7 @@
     blocks, face, sibling, outer = call(
         prepare,
         (perturbation,),
-        whole(1),
+        [pl.BlockSpec((1, nvar // 2, rows, cells), lambda h: (0, h, 0, 0))],
         (
             jax.ShapeDtypeStruct((count, nvar // 2, rows, LANES), jnp.bfloat16),
             jax.ShapeDtypeStruct((ring * 2, 1, LANES), F32),
@@ -191,6 +194,13 @@
         ),
         10**6,
         "prepare",
+        out_specs=[
+            pl.BlockSpec((count // 2, nvar // 2, rows, LANES), lambda h: (h, 0, 0, 0)),
+            pl.BlockSpec((ring * 2, 1, LANES), lambda h: (0, 0, 0)),
+            pl.BlockSpec((nvar, cells), lambda h: (0, 0)),
+            pl.BlockSpec((nvar, cells), lambda h: (0, 0)),
+        ],
+        grid=(2,),
     )
     swaps = [(c, (c + (1 if c % 2 else -1)) % ndom) for c in range(ndom)]
     outer = lax.ppermute(outer, DOM, swaps)
@@ -230,7 +240,7 @@
     )
     return call(
         finish,
-        (total, back, near) + tuple(others) + (select, within),
+        (total, back, near, others[0], others[2], others[1], select, within),
         whole(8),
         (jax.ShapeDtypeStruct(perturbation.shape, F32),),
         3 * nvar * rows * cells,

time: 72.1 us -> 71.7 us (level)
  no operation moved by 1% of the time
where the time goes in v5:
time: 71.7 us; the launch traced here: 71.1 us
  starting transfers between devices  56.4 us (79%)
  waiting for transfers between devices  6.21 us (9%)
  Pallas kernels  4.48 us (6%)
  local copies, waits for them, and re-layouts  2.01 us (3%)
  blocking collectives  1.9 us (3%)
    ppermute x3, starting transfers between devices, shards(): lax.ppermute(near, FAR, [(f, f ^ s) for f in range(far)])  17 us
    all_to_all x1, starting transfers between devices, shards(): got = lax.all_to_all(blocks, INST, 0, 0, tiled=True)  16.5 us
    ppermute x1, starting transfers between devices, shards(): outer = lax.ppermute(outer, DOM, swaps)  11 us
    all_to_all x1, starting transfers between devices, shards(): back = lax.all_to_all(mixed, INST, 0, 0, tiled=True)  7.52 us
    all_to_all x1, waiting for transfers between devices, shards(): near = lax.all_to_all(face, (RING, CORE), 0, 0, tiled=True)  4.66 us
    pallas_call x4, Pallas kernels, call(): pl.pallas_call(body, grid=grid, out_shape=outs, in_specs=specs, out_specs...  4.48 us
    all_to_all x1, starting transfers between devices, shards(): near = lax.all_to_all(face, (RING, CORE), 0, 0, tiled=True)  4.31 us
    unnamed x14, local copies, waits for them, and re-layouts  2.01 us
  transfers between devices with their start and end apart: 7, of which 2 were waited for; matrix products, arithmetic and copies ran while one was open for 0% of the time, Pallas kernels for 4%

profile of v5, /device:TPU:2, one launch (start us, length us, event | category | flops | bytes accessed | tf_op | source)
XLA Modules:
  0.0 71.1 jit_solution(7140635469616009217)
XLA Ops:
  0.0 0.0 copy-start.1
  0.0 1.0 %copy-done.1 = f32[1,6,16,1024]{3,2,1,0:T(8,128)S(1)} copy-done((f32[1,6,16,1024]{3,2,1,0:T(8,128)S(1)}, f32[1,6,16,1024]{3,2,1,0:T(8,128)}, u32[]{:S(2)}) %copy-start.1) | copy-done | bytes 393240
  1.0 0.0 copy-start.3
  1.0 0.0 copy-start.4
  1.0 0.0 copy-start.5
  1.0 0.0 copy-start.6
  1.0 0.9 %prepare.1 = (bf16[16,3,16,128]{3,2,1,0:T(8,128)(2,1)}, f32[16,1,128]{2,1,0:T(1,128)}, f32[6,1024]{1,0:T(8,128)S(1)}, f32[6,1024]{1,0:T(8,128)S(1)}) custom-call(f32[1,6,16,1024]{3,2,1,0:T(8,128)S(1)} %copy-done.1), custom_call_target="tpu_custom_call" | custom-call | flops 1000000 | bytes 647168 | tf_op jit(solution)/shard_map/prepare/pallas_call | solution.py:27
  1.9 16.5 %all-to-all-start.1 = ((bf16[16,3,16,128]{3,2,1,0:T(8,128)(2,1)}), bf16[16,3,16,128]{3,2,1,0:T(8,128)(2,1)S(1)}, u32[]{:S(2)}, u32[]{:S(2)}) async-start(bf16[16,3,16,128]{3,2,1,0:T(8,128)(2,1)} %get-tuple-element.16), calls=%async_computation.1 | async-start | bytes 393216 | tf_op jit(solution)/shard_map/all_to_all | solution.py:209
  18.4 11.0 %collective-permute-start = (f32[6,1024]{1,0:T(8,128)S(1)}, f32[6,1024]{1,0:T(8,128)S(1)}, u32[]{:S(2)}, u32[]{:S(2)}) collective-permute-start(f32[6,1024]{1,0:T(8,128)S(1)} %get-tuple-element.17), channel_id=1, source_target_pairs={{0,63},{1,2},{2,1},{3,4},{4,3},{5,6},{6,5},{7,8},{8,7},{9,10},{10,... | collective-permute-start | bytes 73736 | tf_op jit(solution)/shard_map/ppermute | solution.py:206
  29.5 0.0 all-to-all-done.1.got_ref
  29.5 4.3 %all-to-all-start = ((f32[16,1,128]{2,1,0:T(1,128)}), f32[16,1,128]{2,1,0:T(1,128)S(1)}, u32[]{:S(2)}, u32[]{:S(2)}) async-start(f32[16,1,128]{2,1,0:T(1,128)} %get-tuple-element.15), calls=%async_computation | async-start | bytes 16384 | tf_op jit(solution)/shard_map/all_to_all | solution.py:207
  33.8 1.9 %all-gather.1.pair_ref = f32[2,6,1024]{2,1,0:T(8,128)S(1)} all-gather(f32[1,6,1024]{2,1,0:T(8,128)S(1)} %bitcast.1), channel_id=2, replica_groups=mesh['inst'=16,'ring'=8,'far'=4,'core'=2] {'core'}, dimensions={0}, use_global_device_ids=true | all-gather | bytes 73728 | tf_op jit(solution)/shard_map/all_gather | solution.py:208
  35.7 0.0 collective-permute-done.outer_ref
  35.7 1.0 %mix.1 = f32[16,3,16,128]{3,2,1,0:T(8,128)} custom-call(bf16[16,3,16,128]{3,2,1,0:T(8,128)(2,1)S(1)} %all-to-all-done.1.got_ref, f32[6,1024]{1,0:T(8,128)S(1)} %collective-permute-done.outer_ref, f32[2,6,1024]{2,1,0:T(8,128)S(1)} %all-gather.1.pair_ref), custom_call_target="tpu_custom_call" | custom-call | flops 3145728 | bytes 663552 | tf_op jit(solution)/shard_map/mix/pallas_call | solution.py:27
  36.7 4.7 %all-to-all-done.f0_ref = f32[16,1,128]{2,1,0:T(1,128)S(1)} async-done(((f32[16,1,128]{2,1,0:T(1,128)}), f32[16,1,128]{2,1,0:T(1,128)S(1)}, u32[]{:S(2)}, u32[]{:S(2)}) %all-to-all-start) | async-done | bytes 8224 | tf_op jit(solution)/shard_map/all_to_all | solution.py:207
  41.3 7.5 %all-to-all-start.2 = ((f32[16,3,16,128]{3,2,1,0:T(8,128)}), f32[16,3,16,128]{3,2,1,0:T(8,128)S(1)}, u32[]{:S(2)}, u32[]{:S(2)}) async-start(f32[16,3,16,128]{3,2,1,0:T(8,128)} %mix.1), calls=%async_computation.2 | async-start | bytes 786432 | tf_op jit(solution)/shard_map/all_to_all | solution.py:220
  48.9 8.1 %collective-permute-start.3 = (f32[16,1,128]{2,1,0:T(1,128)S(1)}, f32[16,1,128]{2,1,0:T(1,128)S(1)}, u32[]{:S(2)}, u32[]{:S(2)}) collective-permute-start(f32[16,1,128]{2,1,0:T(1,128)S(1)} %all-to-all-done.f0_ref), channel_id=1, source_target_pairs={{0,4},{2,6},{4,0},{6,2},{1,5},{3,7},{5,1},{7,3},{8,12},{10,14},{12... | collective-permute-start | bytes 24584 | tf_op jit(solution)/shard_map/ppermute | solution.py:219
  57.0 3.6 %collective-permute-start.2 = (f32[16,1,128]{2,1,0:T(1,128)S(1)}, f32[16,1,128]{2,1,0:T(1,128)S(1)}, u32[]{:S(2)}, u32[]{:S(2)}) collective-permute-start(f32[16,1,128]{2,1,0:T(1,128)S(1)} %all-to-all-done.f0_ref), channel_id=1, source_target_pairs={{0,6},{2,4},{4,2},{6,0},{1,7},{3,5},{5,3},{7,1},{8,14},{10,12},{12... | collective-permute-start | bytes 24584 | tf_op jit(solution)/shard_map/ppermute | solution.py:219
  60.6 5.3 %collective-permute-start.1 = (f32[16,1,128]{2,1,0:T(1,128)S(1)}, f32[16,1,128]{2,1,0:T(1,128)S(1)}, u32[]{:S(2)}, u32[]{:S(2)}) collective-permute-start(f32[16,1,128]{2,1,0:T(1,128)S(1)} %all-to-all-done.f0_ref), channel_id=1, source_target_pairs={{0,2},{2,0},{4,6},{6,4},{1,3},{3,1},{5,7},{7,5},{8,10},{10,8},{12,... | collective-permute-start | bytes 24584 | tf_op jit(solution)/shard_map/ppermute | solution.py:219
  65.9 0.0 copy-done
  65.9 0.0 copy-done.3
  65.9 0.0 copy-done.4
  65.9 0.0 copy-done.5
  65.9 0.0 copy-done.6
  66.0 0.0 copy-start.2
  66.0 1.0 %copy-done.2 = f32[1,6,16,1024]{3,2,1,0:T(8,128)S(1)} copy-done((f32[1,6,16,1024]{3,2,1,0:T(8,128)S(1)}, f32[1,6,16,1024]{3,2,1,0:T(8,128)}, u32[]{:S(2)}) %copy-start.2) | copy-done | bytes 393240
  67.0 1.6 %space.1 = (f32[6,16,1024]{2,1,0:T(8,128)S(1)}, f32[2,16,64]{2,1,0:T(8,128)S(1)}, f32[2,16,128]{2,1,0:T(8,128)S(1)}) custom-call(f32[1,6,16,1024]{3,2,1,0:T(8,128)S(1)} %copy-done.2, f32[1,6,6,16,1024]{4,3,2,1,0:T(8,128)S(1)} %copy-done, f32[6,6]{1,0:T(8,128)S(1)} %copy-done.3, f32[6,6]{1,0:T(8,128)S(1)} %copy-done.4, f32[2,6,1024]{2,1,0:T(8,128)S(1)} %all-gather.1.pair_ref, ...), custom_call_target="tpu_custom_call" | custom-call | flops 3538944 | bytes 3244576 | tf_op jit(solution)/shard_map/space/pallas_call | solution.py:27
  68.5 0.0 collective-permute-done.3.f2_ref
  68.5 0.0 collective-permute-done.2.f3_ref
  68.5 1.5 %collective-permute-done.1.f1_ref = f32[16,1,128]{2,1,0:T(1,128)S(1)} collective-permute-done((f32[16,1,128]{2,1,0:T(1,128)S(1)}, f32[16,1,128]{2,1,0:T(1,128)S(1)}, u32[]{:S(2)}, u32[]{:S(2)}) %collective-permute-start.1) | collective-permute-done | bytes 8224 | tf_op jit(solution)/shard_map/ppermute | solution.py:219
  70.1 0.0 all-to-all-done.2.back_ref
  70.1 1.0 %finish.1 = f32[1,6,16,1024]{3,2,1,0:T(8,128)} custom-call(f32[6,16,1024]{2,1,0:T(8,128)S(1)} %get-tuple-element.20.sum_ref, f32[16,3,16,128]{3,2,1,0:T(8,128)S(1)} %all-to-all-done.2.back_ref, f32[16,1,128]{2,1,0:T(1,128)S(1)} %all-to-all-done.f0_ref, f32[16,1,128]{2,1,0:T(1,128)S(1)} %collective-permute-done.1.f1_ref, ...), custom_call_target="tpu_custom_call" | custom-call | flops 294912 | bytes 1236992 | tf_op jit(solution)/shard_map/finish/pallas_call | solution.py:27
  (1 shorter events, 0.0 us)
Async XLA Ops:
  0.0 1.0 %copy-start.1 = (f32[1,6,16,1024]{3,2,1,0:T(8,128)S(1)}, f32[1,6,16,1024]{3,2,1,0:T(8,128)}, u32[]{:S(2)}) copy-start(f32[1,6,16,1024]{3,2,1,0:T(8,128)} %p_hbm.1) | copy-start | bytes 1179652
  1.0 64.9 %copy-start = (f32[1,6,6,16,1024]{4,3,2,1,0:T(8,128)S(1)}, f32[1,6,6,16,1024]{4,3,2,1,0:T(8,128)}, u32[]{:S(2)}) copy-start(f32[1,6,6,16,1024]{4,3,2,1,0:T(8,128)} %jac_hbm.1) | copy-start | bytes 7077892
  1.0 64.9 %copy-start.3 = (f32[6,6]{1,0:T(8,128)S(1)}, f32[6,6]{1,0:T(8,128)}, u32[]{:S(2)}) copy-start(f32[6,6]{1,0:T(8,128)} %theta_hbm.1) | copy-start | bytes 436
  1.0 64.9 %copy-start.4 = (f32[6,6]{1,0:T(8,128)S(1)}, f32[6,6]{1,0:T(8,128)}, u32[]{:S(2)}) copy-start(f32[6,6]{1,0:T(8,128)} %merid_hbm.1) | copy-start | bytes 436
  1.0 64.9 %copy-start.5 = (s32[1,2,16]{2,1,0:T(2,128)S(1)}, s32[1,2,16]{2,1,0:T(2,128)}, u32[]{:S(2)}) copy-start(s32[1,2,16]{2,1,0:T(2,128)} %rows_ref.1) | copy-start | bytes 388
  1.0 64.9 %copy-start.6 = (f32[1,2,16]{2,1,0:T(2,128)S(1)}, f32[1,2,16]{2,1,0:T(2,128)}, u32[]{:S(2)}) copy-start(f32[1,2,16]{2,1,0:T(2,128)} %weights_ref.1) | copy-start | bytes 388
  1.9 27.6 %all-to-all-start.1 = ((bf16[16,3,16,128]{3,2,1,0:T(8,128)(2,1)}), bf16[16,3,16,128]{3,2,1,0:T(8,128)(2,1)S(1)}, u32[]{:S(2)}, u32[]{:S(2)}) async-start(bf16[16,3,16,128]{3,2,1,0:T(8,128)(2,1)} %get-tuple-element.16), calls=%async_computation.1 | async-start | bytes 393216 | tf_op jit(solution)/shard_map/all_to_all | solution.py:209
  18.4 17.3 %collective-permute-start = (f32[6,1024]{1,0:T(8,128)S(1)}, f32[6,1024]{1,0:T(8,128)S(1)}, u32[]{:S(2)}, u32[]{:S(2)}) collective-permute-start(f32[6,1024]{1,0:T(8,128)S(1)} %get-tuple-element.17), channel_id=1, source_target_pairs={{0,63},{1,2},{2,1},{3,4},{4,3},{5,6},{6,5},{7,8},{8,7},{9,10},{10,... | collective-permute-start | bytes 73736 | tf_op jit(solution)/shard_map/ppermute | solution.py:206
  29.5 11.9 %all-to-all-start = ((f32[16,1,128]{2,1,0:T(1,128)}), f32[16,1,128]{2,1,0:T(1,128)S(1)}, u32[]{:S(2)}, u32[]{:S(2)}) async-start(f32[16,1,128]{2,1,0:T(1,128)} %get-tuple-element.15), calls=%async_computation | async-start | bytes 16384 | tf_op jit(solution)/shard_map/all_to_all | solution.py:207
  41.3 28.7 %all-to-all-start.2 = ((f32[16,3,16,128]{3,2,1,0:T(8,128)}), f32[16,3,16,128]{3,2,1,0:T(8,128)S(1)}, u32[]{:S(2)}, u32[]{:S(2)}) async-start(f32[16,3,16,128]{3,2,1,0:T(8,128)} %mix.1), calls=%async_computation.2 | async-start | bytes 786432 | tf_op jit(solution)/shard_map/all_to_all | solution.py:220
  48.9 19.7 %collective-permute-start.3 = (f32[16,1,128]{2,1,0:T(1,128)S(1)}, f32[16,1,128]{2,1,0:T(1,128)S(1)}, u32[]{:S(2)}, u32[]{:S(2)}) collective-permute-start(f32[16,1,128]{2,1,0:T(1,128)S(1)} %all-to-all-done.f0_ref), channel_id=1, source_target_pairs={{0,4},{2,6},{4,0},{6,2},{1,5},{3,7},{5,1},{7,3},{8,12},{10,14},{12... | collective-permute-start | bytes 24584 | tf_op jit(solution)/shard_map/ppermute | solution.py:219
  57.0 11.6 %collective-permute-start.2 = (f32[16,1,128]{2,1,0:T(1,128)S(1)}, f32[16,1,128]{2,1,0:T(1,128)S(1)}, u32[]{:S(2)}, u32[]{:S(2)}) collective-permute-start(f32[16,1,128]{2,1,0:T(1,128)S(1)} %all-to-all-done.f0_ref), channel_id=1, source_target_pairs={{0,6},{2,4},{4,2},{6,0},{1,7},{3,5},{5,3},{7,1},{8,14},{10,12},{12... | collective-permute-start | bytes 24584 | tf_op jit(solution)/shard_map/ppermute | solution.py:219
  60.6 9.5 %collective-permute-start.1 = (f32[16,1,128]{2,1,0:T(1,128)S(1)}, f32[16,1,128]{2,1,0:T(1,128)S(1)}, u32[]{:S(2)}, u32[]{:S(2)}) collective-permute-start(f32[16,1,128]{2,1,0:T(1,128)S(1)} %all-to-all-done.f0_ref), channel_id=1, source_target_pairs={{0,2},{2,0},{4,6},{6,4},{1,3},{3,1},{5,7},{7,5},{8,10},{10,8},{12,... | collective-permute-start | bytes 24584 | tf_op jit(solution)/shard_map/ppermute | solution.py:219
  66.0 1.0 %copy-start.2 = (f32[1,6,16,1024]{3,2,1,0:T(8,128)S(1)}, f32[1,6,16,1024]{3,2,1,0:T(8,128)}, u32[]{:S(2)}) copy-start(f32[1,6,16,1024]{3,2,1,0:T(8,128)} %p_hbm.1) | copy-start | bytes 1179652
